TPU v7x, 32 devices: a whole 2x2x4 slice. The times are simulated.
32 devices in a mesh: tok: 4 (over y, x), blk: 2 (over core), rep: 4 (over z).
Axes of the slice: x: 2, y: 2, z: 4, core: 2. Of those that a mesh axis runs over, the one named last changes fastest.
Arguments:
- block_input: bfloat16 [8448, 2048], P(('tok', 'blk', 'rep')), may hold values from -6 to 6
- cotangent: bfloat16 [8448, 2048], P(('tok', 'blk', 'rep')), may hold values from -6 to 6
- segment_ids: int32 [8448], P('tok'), may hold values from 0 to 2, as said below
- norm_gain: float32 [2048], replicated, may hold values from 0.5 to 1.5
- mlp_gain: float32 [2048], replicated, may hold values from 0.5 to 1.5
- w_input: bfloat16 [2048, 2560], P(('tok', 'blk'), 'rep'), may hold values from -0.125 to 0.125
- w_branch: bfloat16 [2048, 2560], P(('tok', 'blk'), 'rep'), may hold values from -0.125 to 0.125
- w_output: bfloat16 [2560, 2048], P('rep', ('tok', 'blk')), may hold values from -0.3125 to 0.3125
- w_gate: bfloat16 [2048, 6144], P(('tok', 'blk'), 'rep'), may hold values from -0.125 to 0.125
- w_up: bfloat16 [2048, 6144], P(('tok', 'blk'), 'rep'), may hold values from -0.125 to 0.125
- w_down: bfloat16 [6144, 2048], P('rep', ('tok', 'blk')), may hold values from -0.109375 to 0.109375
- gate_a: bfloat16 [4, 2, 2, 160, 160], P('rep', 'blk'), may hold values from -0.5 to 0.5
- gate_i: bfloat16 [4, 2, 2, 160, 160], P('rep', 'blk'), may hold values from -0.5 to 0.5
- conv_weight: float32 [4, 4, 2, 320], P(None, 'rep', 'blk'), may hold values from -3 to 3
- conv_bias: float32 [4, 2, 320], P('rep', 'blk'), may hold values from -3 to 3
- bias_a: float32 [4, 2, 320], P('rep', 'blk'), may hold values from -3 to 3
- bias_i: float32 [4, 2, 320], P('rep', 'blk'), may hold values from -3 to 3
- decay_param: float32 [4, 2, 320], P('rep', 'blk'), may hold values from 2 to 6
Outputs:
- block_out: bfloat16 [8448, 2048], P(('tok', 'blk', 'rep'))
- input_grad: float32 [8448, 2048], P(('tok', 'blk', 'rep'))
- norm_gain_grad: float32 [2048], replicated
- mlp_gain_grad: float32 [2048], replicated
- w_input_grad: float32 [2048, 2560], P(('tok', 'blk'), 'rep')
- w_branch_grad: float32 [2048, 2560], P(('tok', 'blk'), 'rep')
- w_output_grad: float32 [2560, 2048], P('rep', ('tok', 'blk'))
- w_gate_grad: float32 [2048, 6144], P(('tok', 'blk'), 'rep')
- w_up_grad: float32 [2048, 6144], P(('tok', 'blk'), 'rep')
- w_down_grad: float32 [6144, 2048], P('rep', ('tok', 'blk'))
- gate_a_grad: float32 [4, 2, 2, 160, 160], P('rep', 'blk')
- gate_i_grad: float32 [4, 2, 2, 160, 160], P('rep', 'blk')
- conv_weight_grad: float32 [4, 4, 2, 320], P(None, 'rep', 'blk')
- conv_bias_grad: float32 [4, 2, 320], P('rep', 'blk')
- bias_a_grad: float32 [4, 2, 320], P('rep', 'blk')
- bias_i_grad: float32 [4, 2, 320], P('rep', 'blk')
- decay_param_grad: float32 [4, 2, 320], P('rep', 'blk')
Inputs may be any that keep to these rules, and one draw needn't show every extreme that they name: `segment_ids`: within each aligned block of 2112 slots the ids never fall, start at 0, take every value up to 2, and the slots with id 2 are the block's tail (padding, at least one slot).
All inputs are finite; a program needn't handle non-finite values.
Results may differ from a plain program's by a relative error of at most 0.01.
Values may be sent and summed in bfloat16 or wider, within the bound.
No kernel may reach another device: no remote copies, remote signals or barrier semaphores. Data moves between devices by JAX's collectives and lax.ppermute only.
A program may use at most 256 MiB of HBM per device.

v0:
```python
from functools import partial

import jax
import jax.numpy as jnp
from jax import lax
from jax.sharding import PartitionSpec as P

SEQS = 2


epsilon = 1e-06
gate_power = 8.0
block_steps = 16


def times_transposed(left_op, right_op):
    return lax.dot_general(
        left_op, right_op, (((1,), (1,)), ((), ())), preferred_element_type=jnp.float32
    )


def transposed_times(left_op, right_op):
    return lax.dot_general(
        left_op, right_op, (((0,), (0,)), ((), ())), preferred_element_type=jnp.float32
    )


def normalize(values, gain_vec):
    inverse = lax.rsqrt(jnp.mean(values * values, axis=-1, keepdims=True) + epsilon)
    scaled = values * inverse
    return (scaled * gain_vec, scaled, inverse)


def normalize_back(grad_in, gain_vec, scaled, inverse):
    weighted = grad_in * gain_vec
    through = inverse * (weighted - scaled * jnp.mean(weighted * scaled, axis=-1, keepdims=True))
    return (through, jnp.sum(grad_in * scaled, axis=0))


def same_masks(bucket_ids, tap_count):
    length = bucket_ids.shape[0]
    same_list = [jnp.ones((length,), jnp.float32)]
    for lag_step in range(1, tap_count):
        earlier = jnp.concatenate(
            [jnp.full((lag_step,), -1, jnp.int32), bucket_ids[: length - lag_step]]
        )
        same_list.append((earlier == bucket_ids).astype(jnp.float32))
    return same_list


def convolve(values, weights, bias_vec, same_list):
    length = values.shape[0]
    summed = bias_vec + weights[0] * values
    for lag_step in range(1, len(same_list)):
        shifted = jnp.concatenate(
            [jnp.zeros((lag_step, values.shape[1]), values.dtype), values[: length - lag_step]],
            axis=0,
        )
        summed = summed + weights[lag_step] * shifted * same_list[lag_step][:, None]
    return summed


def blocked_states(decays, driven):
    length, channels = decays.shape
    block_count = length // block_steps
    rates = decays.reshape(block_count, block_steps, channels)
    pushes = driven.reshape(block_count, block_steps, channels)
    running = jnp.zeros((block_count, channels), jnp.float32)
    carried_rate = jnp.ones((block_count, channels), jnp.float32)
    local_list = []
    rate_list = []
    for step_index in range(block_steps):
        running = rates[:, step_index] * running + pushes[:, step_index]
        carried_rate = rates[:, step_index] * carried_rate
        local_list.append(running)
        rate_list.append(carried_rate)
    local_states = jnp.stack(local_list, axis=1)
    local_rates = jnp.stack(rate_list, axis=1)

    def combine(early_pair, late_pair):
        return (early_pair[0] * late_pair[0], late_pair[0] * early_pair[1] + late_pair[1])

    block_ends = lax.associative_scan(combine, (carried_rate, running), axis=0)[1]
    entering = jnp.concatenate(
        [jnp.zeros((1, channels), jnp.float32), block_ends[: block_count - 1]], axis=0
    )
    whole = local_states + local_rates * entering[:, None, :]
    return whole.reshape(length, channels)


def recurrence(mixed_a, mixed_i, conv_out, bias_a, bias_i, decay_param, keep_prev):
    gate_r = jax.nn.sigmoid(mixed_a + bias_a)
    gate_in = jax.nn.sigmoid(mixed_i + bias_i)
    log_a = -gate_power * jax.nn.softplus(-decay_param) * gate_r
    decays = jnp.exp(log_a) * keep_prev[:, None]
    driven = jnp.sqrt(-jnp.expm1(2.0 * log_a)) * gate_in * conv_out
    return blocked_states(decays, driven)


def spread_rows(values):
    return lax.all_gather(values, "rep", axis=0, tiled=True)


def collect_rows(values):
    return lax.psum_scatter(values, "rep", scatter_dimension=0, tiled=True)


def into_mixer(values):
    return lax.all_to_all(values, "blk", split_axis=1, concat_axis=0, tiled=True)


def out_of_mixer(values):
    return lax.all_to_all(values, "blk", split_axis=0, concat_axis=1, tiled=True)


def gather_weights(w_input, w_branch, w_gate, w_up, w_output, w_down):
    row_parts = (
        lax.all_gather(w_input, ("tok", "blk"), axis=0, tiled=True),
        lax.all_gather(w_branch, ("tok", "blk"), axis=0, tiled=True),
        lax.all_gather(w_gate, ("tok", "blk"), axis=0, tiled=True),
        lax.all_gather(w_up, ("tok", "blk"), axis=0, tiled=True),
    )
    column_parts = (
        lax.all_gather(w_output, ("tok", "blk"), axis=1, tiled=True),
        lax.all_gather(w_down, ("tok", "blk"), axis=1, tiled=True),
    )
    return tuple(row_parts) + tuple(column_parts)


def body(
    block_input,
    cotangent,
    segment_ids,
    norm_gain,
    mlp_gain,
    w_input,
    w_branch,
    w_output,
    w_gate,
    w_up,
    w_down,
    gate_a,
    gate_i,
    conv_weight,
    conv_bias,
    bias_a,
    bias_i,
    decay_param,
):
    row_count = block_input.shape[0]
    full_in, full_branch, full_gate, full_up, full_out, full_down = gather_weights(
        w_input, w_branch, w_gate, w_up, w_output, w_down
    )
    x_first = block_input.astype(jnp.float32)
    normed1, scaled1, inverse1 = normalize(x_first, norm_gain)
    gathered1 = spread_rows(normed1.astype(jnp.bfloat16))
    mixer_in = jnp.dot(gathered1, full_in, preferred_element_type=jnp.float32).astype(jnp.bfloat16)
    branch = jnp.dot(gathered1, full_branch, preferred_element_type=jnp.float32)
    bucket_in = into_mixer(mixer_in).astype(jnp.float32)
    length, channels = bucket_in.shape
    tap_count = conv_weight.shape[0]
    blocks = gate_a.shape[2]
    block_width = gate_a.shape[3]
    same_list = same_masks(segment_ids, tap_count)
    conv_w = conv_weight.reshape(tap_count, channels)
    conv_b = conv_bias.reshape(channels)
    local_bias_a = bias_a.reshape(channels)
    local_bias_i = bias_i.reshape(channels)
    local_decay = decay_param.reshape(channels)
    local_a = gate_a.reshape(blocks, block_width, block_width)
    local_i = gate_i.reshape(blocks, block_width, block_width)

    def conv_piece(values, weights, bias_vec):
        return convolve(values, weights, bias_vec, same_list)

    conv_out, conv_back = jax.vjp(conv_piece, bucket_in, conv_w, conv_b)
    conv_low = conv_out.astype(jnp.bfloat16).reshape(length, blocks, block_width)
    mixed_a = jnp.einsum(
        "lgi,gio->lgo", conv_low, local_a, preferred_element_type=jnp.float32
    ).reshape(length, channels)
    mixed_i = jnp.einsum(
        "lgi,gio->lgo", conv_low, local_i, preferred_element_type=jnp.float32
    ).reshape(length, channels)
    states, states_back = jax.vjp(
        partial(recurrence, keep_prev=same_list[1]),
        mixed_a,
        mixed_i,
        conv_out,
        local_bias_a,
        local_bias_i,
        local_decay,
    )
    states_rows = out_of_mixer(states.astype(jnp.bfloat16)).astype(jnp.float32)
    activated, branch_back = jax.vjp(jax.nn.gelu, branch)
    merged = (activated * states_rows).astype(jnp.bfloat16)
    residual = x_first + collect_rows(jnp.dot(merged, full_out, preferred_element_type=jnp.float32))
    normed2, scaled2, inverse2 = normalize(residual, mlp_gain)
    gathered2 = spread_rows(normed2.astype(jnp.bfloat16))
    gate_pre = jnp.dot(gathered2, full_gate, preferred_element_type=jnp.float32)
    up_pre = jnp.dot(gathered2, full_up, preferred_element_type=jnp.float32)
    gate_act, gate_back = jax.vjp(jax.nn.gelu, gate_pre)
    hidden = (gate_act * up_pre).astype(jnp.bfloat16)
    final_rows = residual + collect_rows(
        jnp.dot(hidden, full_down, preferred_element_type=jnp.float32)
    )
    block_out = final_rows.astype(jnp.bfloat16)
    back_in, back_branch, back_gate, back_up, back_out, back_down = gather_weights(
        w_input, w_branch, w_gate, w_up, w_output, w_down
    )
    offset = (lax.axis_index("blk") * lax.axis_size("rep") + lax.axis_index("rep")) * row_count
    own_ids = lax.dynamic_slice_in_dim(segment_ids, offset, row_count)
    grad_final = cotangent.astype(jnp.float32) * (own_ids < SEQS).astype(jnp.float32)[:, None]
    down_rows = spread_rows(grad_final.astype(jnp.bfloat16))
    grad_hidden = times_transposed(down_rows, back_down)
    term_down = transposed_times(hidden, down_rows)
    grad_gate = gate_back(grad_hidden * up_pre)[0].astype(jnp.bfloat16)
    grad_up = (grad_hidden * gate_act).astype(jnp.bfloat16)
    term_gate = transposed_times(gathered2, grad_gate)
    term_up = transposed_times(gathered2, grad_up)
    grad_normed2 = collect_rows(
        times_transposed(grad_gate, back_gate) + times_transposed(grad_up, back_up)
    )
    through2, gain2_term = normalize_back(grad_normed2, mlp_gain, scaled2, inverse2)
    grad_residual = grad_final + through2
    mixer_rows = spread_rows(grad_residual.astype(jnp.bfloat16))
    grad_merged = times_transposed(mixer_rows, back_out)
    term_out = transposed_times(merged, mixer_rows)
    grad_branch = branch_back(grad_merged * states_rows)[0].astype(jnp.bfloat16)
    grad_states = into_mixer((grad_merged * activated).astype(jnp.bfloat16)).astype(jnp.float32)
    grad_mixed_a, grad_mixed_i, grad_direct, grad_bias_a, grad_bias_i, grad_decay = states_back(
        grad_states
    )
    low_mixed_a = grad_mixed_a.astype(jnp.bfloat16).reshape(length, blocks, block_width)
    low_mixed_i = grad_mixed_i.astype(jnp.bfloat16).reshape(length, blocks, block_width)
    grad_gate_a = jnp.einsum(
        "lgi,lgo->gio", conv_low, low_mixed_a, preferred_element_type=jnp.float32
    )
    grad_gate_i = jnp.einsum(
        "lgi,lgo->gio", conv_low, low_mixed_i, preferred_element_type=jnp.float32
    )
    through_gates = jnp.einsum(
        "lgo,gio->lgi", low_mixed_a, local_a, preferred_element_type=jnp.float32
    ) + jnp.einsum("lgo,gio->lgi", low_mixed_i, local_i, preferred_element_type=jnp.float32)
    grad_conv = grad_direct + through_gates.reshape(length, channels)
    grad_bucket, grad_conv_w, grad_conv_b = conv_back(grad_conv)
    grad_mixer_in = out_of_mixer(grad_bucket.astype(jnp.bfloat16))
    term_in = transposed_times(gathered1, grad_mixer_in)
    term_branch = transposed_times(gathered1, grad_branch)
    grad_normed1 = collect_rows(
        times_transposed(grad_mixer_in, back_in) + times_transposed(grad_branch, back_branch)
    )
    through1, gain1_term = normalize_back(grad_normed1, norm_gain, scaled1, inverse1)
    input_grad = grad_residual + through1
    gain1_grad, gain2_grad = lax.psum((gain1_term, gain2_term), ("tok", "blk", "rep"))
    grad_in_w, grad_branch_w, grad_gate_w, grad_up_w = (
        lax.psum_scatter(term_in, ("tok", "blk"), scatter_dimension=0, tiled=True),
        lax.psum_scatter(term_branch, ("tok", "blk"), scatter_dimension=0, tiled=True),
        lax.psum_scatter(term_gate, ("tok", "blk"), scatter_dimension=0, tiled=True),
        lax.psum_scatter(term_up, ("tok", "blk"), scatter_dimension=0, tiled=True),
    )
    grad_out_w, grad_down_w = (
        lax.psum_scatter(term_out, ("tok", "blk"), scatter_dimension=1, tiled=True),
        lax.psum_scatter(term_down, ("tok", "blk"), scatter_dimension=1, tiled=True),
    )
    summed_a, summed_i, summed_cw, summed_cb, summed_ba, summed_bi, summed_decay = lax.psum(
        (
            grad_gate_a.reshape(gate_a.shape),
            grad_gate_i.reshape(gate_i.shape),
            grad_conv_w.reshape(conv_weight.shape),
            grad_conv_b.reshape(conv_bias.shape),
            grad_bias_a.reshape(bias_a.shape),
            grad_bias_i.reshape(bias_i.shape),
            grad_decay.reshape(decay_param.shape),
        ),
        "tok",
    )
    return (
        block_out,
        input_grad,
        gain1_grad,
        gain2_grad,
        grad_in_w,
        grad_branch_w,
        grad_out_w,
        grad_gate_w,
        grad_up_w,
        grad_down_w,
        summed_a,
        summed_i,
        summed_cw,
        summed_cb,
        summed_ba,
        summed_bi,
        summed_decay,
    )


def solution(mesh):
    return jax.shard_map(
        body,
        mesh=mesh,
        in_specs=(
            P(("tok", "blk", "rep"), None),
            P(("tok", "blk", "rep"), None),
            P("tok"),
            P(),
            P(),
            P(("tok", "blk"), "rep"),
            P(("tok", "blk"), "rep"),
            P("rep", ("tok", "blk")),
            P(("tok", "blk"), "rep"),
            P(("tok", "blk"), "rep"),
            P("rep", ("tok", "blk")),
            P("rep", "blk", None, None, None),
            P("rep", "blk", None, None, None),
            P(None, "rep", "blk", None),
            P("rep", "blk", None),
            P("rep", "blk", None),
            P("rep", "blk", None),
            P("rep", "blk", None),
        ),
        out_specs=(
            P(("tok", "blk", "rep"), None),
            P(("tok", "blk", "rep"), None),
            P(),
            P(),
            P(("tok", "blk"), "rep"),
            P(("tok", "blk"), "rep"),
            P("rep", ("tok", "blk")),
            P(("tok", "blk"), "rep"),
            P(("tok", "blk"), "rep"),
            P("rep", ("tok", "blk")),
            P("rep", "blk", None, None, None),
            P("rep", "blk", None, None, None),
            P(None, "rep", "blk", None),
            P("rep", "blk", None),
            P("rep", "blk", None),
            P("rep", "blk", None),
            P("rep", "blk", None),
        ),
        check_vma=False,
    )
```

profile of v0, /device:TPU:0, one launch (start us, length us, event | category | flops | bytes accessed | tf_op | source)
XLA Modules:
  0.0 2058.1 jit_solution(5903831997673918141)
XLA Ops:
  15.1 27.8 %all-gather.15.cloned.1.call-done = bf16[2048,640]{1,0:T(8,128)(2,1)} async-done(((bf16[256,640]{1,0:T(8,128)(2,1)}), bf16[2048,640]{1,0:T(8,128)(2,1)}) %all-gather.15.cloned.1.call-update) | async-done | bytes 2621456 | tf_op jit(solution)/shard_map/all_gather | solution.py:118
  42.8 85.1 %all-gather.11.cloned.1.call-done = bf16[1056,2048]{1,0:T(8,128)(2,1)} async-done(((bf16[264,2048]{1,0:T(8,128)(2,1)}), bf16[1056,2048]{1,0:T(8,128)(2,1)}) %all-gather.11.cloned.1.call-update) | async-done | bytes 4325392 | tf_op jit(solution)/shard_map/all_gather | solution.py:101
  127.9 6.6 convolution_convert_fusion
  154.9 5.3 copy.132
  160.3 6.4 reshape.287
  180.2 6.5 fusion.117
  191.3 11.5 fusion.150
  323.3 9.2 multiply_convert_fusion.3
  332.6 8.0 fusion.169
  341.2 146.1 %reduce-scatter.11.cloned.1.call-done = f32[264,2048]{1,0:T(8,128)} async-done(((f32[1056,2048]{1,0:T(8,128)}), f32[264,2048]{1,0:T(8,128)}) %reduce-scatter.11.cloned.1.call-update) | async-done | bytes 2162704 | tf_op jit(solution)/shard_map/reduce_scatter | solution.py:105
  493.3 42.1 %all-gather.23.cloned.1.call-done = bf16[2048,1536]{1,0:T(8,128)(2,1)} async-done(((bf16[256,1536]{1,0:T(8,128)(2,1)}), bf16[2048,1536]{1,0:T(8,128)(2,1)}) %all-gather.23.cloned.1.call-update) | async-done | bytes 6291472 | tf_op jit(solution)/shard_map/all_gather | solution.py:121
  535.4 85.1 %all-gather.19.cloned.1.call-done = bf16[1056,2048]{1,0:T(8,128)(2,1)} async-done(((bf16[264,2048]{1,0:T(8,128)(2,1)}), bf16[1056,2048]{1,0:T(8,128)(2,1)}) %all-gather.19.cloned.1.call-update) | async-done | bytes 4325392 | tf_op jit(solution)/shard_map/all_gather | solution.py:101
  620.5 12.2 fusion.171
  632.7 33.7 %all-gather.21.cloned.1.call-done = bf16[2048,1536]{1,0:T(8,128)(2,1)} async-done(((bf16[256,1536]{1,0:T(8,128)(2,1)}), bf16[2048,1536]{1,0:T(8,128)(2,1)}) %all-gather.21.cloned.1.call-update) | async-done | bytes 6291472 | tf_op jit(solution)/shard_map/all_gather | solution.py:120
  666.5 12.1 fusion.170
  678.6 73.0 %all-gather.27.cloned.1.call-done = bf16[1056,2048]{1,0:T(8,128)(2,1)} async-done(((bf16[264,2048]{1,0:T(8,128)(2,1)}), bf16[1056,2048]{1,0:T(8,128)(2,1)}) %all-gather.27.cloned.1.call-update) | async-done | bytes 4325392 | tf_op jit(solution)/shard_map/all_gather | solution.py:101
  751.6 46.9 %all-gather.25.cloned.1.call-done = bf16[1536,2048]{1,0:T(8,128)(2,1)} async-done(((bf16[1536,256]{1,0:T(8,128)(2,1)}), bf16[1536,2048]{1,0:T(8,128)(2,1)}) %all-gather.25.cloned.1.call-update) | async-done | bytes 6291472 | tf_op jit(solution)/shard_map/all_gather | solution.py:125
  798.5 20.2 multiply_convert_fusion
  818.7 8.9 fusion.173
  827.6 12.2 convolution_add_fusion
  839.9 12.0 fusion.172
  852.0 136.6 %reduce-scatter.15.cloned.1.call-done = f32[264,2048]{1,0:T(8,128)} async-done(((f32[1056,2048]{1,0:T(8,128)}), f32[264,2048]{1,0:T(8,128)}) %reduce-scatter.15.cloned.1.call-update) | async-done | bytes 2162704 | tf_op jit(solution)/shard_map/reduce_scatter | solution.py:105
  991.4 148.9 %reduce-scatter.13.cloned.1.call-done = f32[264,2048]{1,0:T(8,128)} async-done(((f32[1056,2048]{1,0:T(8,128)}), f32[264,2048]{1,0:T(8,128)}) %reduce-scatter.13.cloned.1.call-update) | async-done | bytes 2162704 | tf_op jit(solution)/shard_map/reduce_scatter | solution.py:105
  1140.3 5.1 fusion.146
  1147.4 5.1 reshape.311
  1152.6 76.8 %all-gather.29.cloned.1.call-done = bf16[1056,2048]{1,0:T(8,128)(2,1)} async-done(((bf16[264,2048]{1,0:T(8,128)(2,1)}), bf16[1056,2048]{1,0:T(8,128)(2,1)}) %all-gather.29.cloned.1.call-update) | async-done | bytes 4325392 | tf_op jit(solution)/shard_map/all_gather | solution.py:101
  1229.3 10.4 fusion.34
  1252.8 6.0 broadcast_multiply_fusion
  1322.7 8.7 fusion.119
  1334.5 7.7 copy.199
  1342.3 8.5 fusion.118
  1371.3 5.8 convolution_add_fusion.1
  1377.2 13.7 fusion.180
  1391.0 14.0 fusion.179
  1405.1 13.8 fusion.178
  1424.2 8.6 fusion.177
  1434.2 8.7 fusion.176
  1444.4 8.8 fusion.175
  1455.7 16.5 all-reduce.127
  1472.2 52.2 %reduce-scatter.17.cloned.1.call-done = f32[264,2048]{1,0:T(8,128)} async-done(((f32[1056,2048]{1,0:T(8,128)}), f32[264,2048]{1,0:T(8,128)}) %reduce-scatter.17.cloned.1.call-update) | async-done | bytes 2162704 | tf_op jit(solution)/shard_map/reduce_scatter | solution.py:105
  1526.9 41.5 %all-reduce.126 = (f32[2048]{0:T(1024)}, f32[2048]{0:T(1024)}) all-reduce(f32[2048]{0:T(1024)S(1)} %get-tuple-element.21, f32[2048]{0:T(1024)S(1)} %copy-done.192), channel_id=1, replica_groups=mesh['tok'=4,'blk'=2,'rep'=4] {'tok','blk','rep'}, use_global_device_ids=true, to_apply=%region_10.11 | all-reduce | flops 4096 | bytes 32768 | tf_op jit(solution)/shard_map/psum | solution.py:254
  1571.9 50.3 %reduce-scatter.29.cloned.1.call-done = f32[1536,256]{1,0:T(8,128)} async-done(((f32[1536,2048]{1,0:T(8,128)}), f32[1536,256]{1,0:T(8,128)}) %reduce-scatter.29.cloned.1.call-update) | async-done | bytes 1572880 | tf_op jit(solution)/shard_map/reduce_scatter | solution.py:263
  1622.2 96.4 %reduce-scatter.27.cloned.1.call-done = f32[256,1536]{1,0:T(8,128)} async-done(((f32[2048,1536]{1,0:T(8,128)}), f32[256,1536]{1,0:T(8,128)}) %reduce-scatter.27.cloned.1.call-update) | async-done | bytes 1572880 | tf_op jit(solution)/shard_map/reduce_scatter | solution.py:259
  1718.6 96.4 %reduce-scatter.25.cloned.1.call-done = f32[256,1536]{1,0:T(8,128)} async-done(((f32[2048,1536]{1,0:T(8,128)}), f32[256,1536]{1,0:T(8,128)}) %reduce-scatter.25.cloned.1.call-update) | async-done | bytes 1572880 | tf_op jit(solution)/shard_map/reduce_scatter | solution.py:258
  1814.9 50.5 %all-reduce.131.cloned.1.call-done = (f32[1,1,2,160,160]{4,3,2,1,0:T(8,128)}, f32[1,1,2,160,160]{4,3,2,1,0:T(8,128)}) async-done(((f32[1,1,2,160,160]{4,3,2,1,0:T(8,128)}, f32[1,1,2,160,160]{4,3,2,1,0:T(8,128)}), (f32[1,1,2,160,160]{4,3,2,1,0:T(8,128)}, f32[1,1,2,160,160]{4,3,2,1,0:T(8,128)})) %all-reduce.131.cloned.1.call-update) | async-done | bytes 409616 | tf_op jit(solution)/shard_map/psum | solution.py:265
  1865.5 60.6 %reduce-scatter.23.cloned.1.call-done = f32[640,256]{1,0:T(8,128)} async-done(((f32[640,2048]{1,0:T(8,128)}), f32[640,256]{1,0:T(8,128)}) %reduce-scatter.23.cloned.1.call-update) | async-done | bytes 655376 | tf_op jit(solution)/shard_map/reduce_scatter | solution.py:262
  1926.0 60.8 %reduce-scatter.21.cloned.1.call-done = f32[256,640]{1,0:T(8,128)} async-done(((f32[2048,640]{1,0:T(8,128)}), f32[256,640]{1,0:T(8,128)}) %reduce-scatter.21.cloned.1.call-update) | async-done | bytes 655376 | tf_op jit(solution)/shard_map/reduce_scatter | solution.py:257
  1986.8 60.6 %reduce-scatter.19.cloned.1.call-done = f32[256,640]{1,0:T(8,128)} async-done(((f32[2048,640]{1,0:T(8,128)}), f32[256,640]{1,0:T(8,128)}) %reduce-scatter.19.cloned.1.call-update) | async-done | bytes 655376 | tf_op jit(solution)/shard_map/reduce_scatter | solution.py:256
  (775 shorter events, 296.4 us)
Async XLA Ops:
  7.2 171.6 %copy-start = (bf16[1,1,2,160,160]{4,3,2,1,0:T(8,128)(2,1)S(1)}, bf16[1,1,2,160,160]{4,3,2,1,0:T(8,128)(2,1)}, u32[]{:S(2)}) copy-start(bf16[1,1,2,160,160]{4,3,2,1,0:T(8,128)(2,1)} %param.30) | copy-start | bytes 307204
  7.3 35.6 %all-gather.15.cloned.1.call-start = ((), (), s32[]{:S(2)}) async-start(), calls=%async_computation.16 | async-start | bytes 2949120 | tf_op jit(solution)/shard_map/all_gather | solution.py:118
  8.0 119.9 %all-gather.11.cloned.1.call-start = ((), (), s32[]{:S(2)}) async-start(), calls=%async_computation.14 | async-start | bytes 5406720 | tf_op jit(solution)/shard_map/all_gather | solution.py:101
  12.7 310.7 %all-gather.13.cloned.1.call-start = ((), (), s32[]{:S(2)}) async-start(), calls=%async_computation.15 | async-start | bytes 2949120 | tf_op jit(solution)/shard_map/all_gather | solution.py:119
  13.4 319.1 %all-gather.17.cloned.1.call-start = ((), (), s32[]{:S(2)}) async-start(), calls=%async_computation.17 | async-start | bytes 2949120 | tf_op jit(solution)/shard_map/all_gather | solution.py:124
  14.0 473.3 %reduce-scatter.11.cloned.1.call-start = ((), (), s32[]{:S(2)}) async-start(), calls=%async_computation.18 | async-start | bytes 10813440 | tf_op jit(solution)/shard_map/reduce_scatter | solution.py:105
  14.1 165.3 %copy-start.187 = (f32[320]{0:T(512)}, f32[320]{0:T(512)S(1)}, u32[]{:S(2)}) copy-start(f32[320]{0:T(512)S(1)} %reduce.9) | copy-start | bytes 3844
  14.1 165.3 %copy-start.193 = (f32[320]{0:T(512)}, f32[320]{0:T(512)S(1)}, u32[]{:S(2)}) copy-start(f32[320]{0:T(512)S(1)} %reduce.8) | copy-start | bytes 3844
  14.8 164.7 %copy-start.185 = (f32[320]{0:T(512)}, f32[320]{0:T(512)S(1)}, u32[]{:S(2)}) copy-start(f32[320]{0:T(512)S(1)} %fusion.104) | copy-start | bytes 3844
  14.8 134.1 %copy-start.205 = (f32[320]{0:T(512)}, f32[320]{0:T(512)S(1)}, u32[]{:S(2)}) copy-start(f32[320]{0:T(512)S(1)} %get-tuple-element.28) | copy-start | bytes 3844
  14.8 134.1 %copy-start.207 = (f32[320]{0:T(512)}, f32[320]{0:T(512)S(1)}, u32[]{:S(2)}) copy-start(f32[320]{0:T(512)S(1)} %get-tuple-element.26) | copy-start | bytes 3844
  14.9 134.1 %copy-start.209 = (f32[320]{0:T(512)}, f32[320]{0:T(512)S(1)}, u32[]{:S(2)}) copy-start(f32[320]{0:T(512)S(1)} %get-tuple-element.27) | copy-start | bytes 3844
  14.9 134.1 %copy-start.213 = (f32[320]{0:T(512)}, f32[320]{0:T(512)S(1)}, u32[]{:S(2)}) copy-start(f32[320]{0:T(512)S(1)} %get-tuple-element.25) | copy-start | bytes 3844
  15.0 134.0 %copy-start.157 = (f32[2112]{0:T(1024)}, f32[2112]{0:T(1024)S(1)}, u32[]{:S(2)}) copy-start(f32[2112]{0:T(1024)S(1)} %get-tuple-element.291) | copy-start | bytes 25348
  15.0 134.0 %copy-start.169 = (f32[2112]{0:T(1024)}, f32[2112]{0:T(1024)S(1)}, u32[]{:S(2)}) copy-start(f32[2112]{0:T(1024)S(1)} %get-tuple-element.292) | copy-start | bytes 25348
  15.0 134.0 %copy-start.171 = (f32[2112]{0:T(1024)}, f32[2112]{0:T(1024)S(1)}, u32[]{:S(2)}) copy-start(f32[2112]{0:T(1024)S(1)} %get-tuple-element.293) | copy-start | bytes 25348
  171.9 128.9 %copy-start.15 = (f32[132,1,320]{2,1,0:T(1,128)}, f32[132,1,320]{2,1,0:T(1,128)S(1)}, u32[]{:S(2)}) copy-start(f32[132,1,320]{2,1,0:T(1,128)S(1)} %get-tuple-element.173) | copy-start | bytes 506884
  171.9 128.9 %copy-start.17 = (f32[132,1,320]{2,1,0:T(1,128)}, f32[132,1,320]{2,1,0:T(1,128)S(1)}, u32[]{:S(2)}) copy-start(f32[132,1,320]{2,1,0:T(1,128)S(1)} %get-tuple-element.174) | copy-start | bytes 506884
  171.9 128.9 %copy-start.19 = (f32[132,1,320]{2,1,0:T(1,128)}, f32[132,1,320]{2,1,0:T(1,128)S(1)}, u32[]{:S(2)}) copy-start(f32[132,1,320]{2,1,0:T(1,128)S(1)} %get-tuple-element.172) | copy-start | bytes 506884
  171.9 131.6 %copy-start.23 = (f32[132,1,320]{2,1,0:T(1,128)}, f32[132,1,320]{2,1,0:T(1,128)S(1)}, u32[]{:S(2)}) copy-start(f32[132,1,320]{2,1,0:T(1,128)S(1)} %get-tuple-element.170) | copy-start | bytes 506884
  171.9 133.1 %copy-start.27 = (f32[132,1,320]{2,1,0:T(1,128)}, f32[132,1,320]{2,1,0:T(1,128)S(1)}, u32[]{:S(2)}) copy-start(f32[132,1,320]{2,1,0:T(1,128)S(1)} %get-tuple-element.168) | copy-start | bytes 506884
  171.9 134.6 %copy-start.29 = (f32[132,1,320]{2,1,0:T(1,128)}, f32[132,1,320]{2,1,0:T(1,128)S(1)}, u32[]{:S(2)}) copy-start(f32[132,1,320]{2,1,0:T(1,128)S(1)} %get-tuple-element.166) | copy-start | bytes 506884
  172.0 136.2 %copy-start.31 = (f32[132,1,320]{2,1,0:T(1,128)}, f32[132,1,320]{2,1,0:T(1,128)S(1)}, u32[]{:S(2)}) copy-start(f32[132,1,320]{2,1,0:T(1,128)S(1)} %get-tuple-element.164) | copy-start | bytes 506884
  172.0 137.7 %copy-start.33 = (f32[132,1,320]{2,1,0:T(1,128)}, f32[132,1,320]{2,1,0:T(1,128)S(1)}, u32[]{:S(2)}) copy-start(f32[132,1,320]{2,1,0:T(1,128)S(1)} %get-tuple-element.162) | copy-start | bytes 506884
  172.0 139.2 %copy-start.25 = (f32[132,1,320]{2,1,0:T(1,128)}, f32[132,1,320]{2,1,0:T(1,128)S(1)}, u32[]{:S(2)}) copy-start(f32[132,1,320]{2,1,0:T(1,128)S(1)} %get-tuple-element.175) | copy-start | bytes 506884
  224.7 75.1 %copy-start.155 = (f32[16,320]{1,0:T(8,128)}, f32[16,320]{1,0:T(8,128)S(1)}, u32[]{:S(2)}) copy-start(f32[16,320]{1,0:T(8,128)S(1)} %slice.413) | copy-start | bytes 61444
  340.5 146.8 %copy-start.9 = (bf16[264,2048]{1,0:T(8,128)(2,1)S(1)}, bf16[264,2048]{1,0:T(8,128)(2,1)}, u32[]{:S(2)}) copy-start(bf16[264,2048]{1,0:T(8,128)(2,1)} %param.18) | copy-start | bytes 3244036
  340.6 194.8 %all-gather.23.cloned.1.call-start = ((), (), s32[]{:S(2)}) async-start(), calls=%async_computation.21 | async-start | bytes 7077888 | tf_op jit(solution)/shard_map/all_gather | solution.py:121
  341.1 148.2 %copy-start.180 = (f32[2048]{0:T(1024)S(1)}, f32[2048]{0:T(1024)}, u32[]{:S(2)}) copy-start(f32[2048]{0:T(1024)} %param.22) | copy-start | bytes 24580
  341.2 279.4 %all-gather.19.cloned.1.call-start = ((), (), s32[]{:S(2)}) async-start(), calls=%async_computation.19 | async-start | bytes 5406720 | tf_op jit(solution)/shard_map/all_gather | solution.py:101
  490.6 175.9 %all-gather.21.cloned.1.call-start = ((), (), s32[]{:S(2)}) async-start(), calls=%async_computation.20 | async-start | bytes 7077888 | tf_op jit(solution)/shard_map/all_gather | solution.py:120
  491.3 260.3 %all-gather.27.cloned.1.call-start = ((), (), s32[]{:S(2)}) async-start(), calls=%async_computation.24 | async-start | bytes 5406720 | tf_op jit(solution)/shard_map/all_gather | solution.py:101
  492.7 305.8 %all-gather.25.cloned.1.call-start = ((), (), s32[]{:S(2)}) async-start(), calls=%async_computation.22 | async-start | bytes 7077888 | tf_op jit(solution)/shard_map/all_gather | solution.py:125
  493.3 495.3 %reduce-scatter.15.cloned.1.call-start = ((), (), s32[]{:S(2)}) async-start(), calls=%async_computation.25 | async-start | bytes 10813440 | tf_op jit(solution)/shard_map/reduce_scatter | solution.py:105
  839.8 300.5 %reduce-scatter.13.cloned.1.call-start = ((), (), s32[]{:S(2)}) async-start(), calls=%async_computation.23 | async-start | bytes 10813440 | tf_op jit(solution)/shard_map/reduce_scatter | solution.py:105
  851.9 377.4 %all-gather.29.cloned.1.call-start = ((), (), s32[]{:S(2)}) async-start(), calls=%async_computation.26 | async-start | bytes 5406720 | tf_op jit(solution)/shard_map/all_gather | solution.py:101
  991.4 154.1 %copy-start.212 = (f32[320]{0:T(512)S(1)}, f32[320]{0:T(512)}, u32[]{:S(2)}) copy-start(f32[320]{0:T(512)} %copy-done.211) | copy-start | bytes 3844
  991.4 154.2 %copy-start.194 = (f32[320]{0:T(512)S(1)}, f32[320]{0:T(512)}, u32[]{:S(2)}) copy-start(f32[320]{0:T(512)} %copy-done.193) | copy-start | bytes 3844
  991.4 154.8 %copy-start.188 = (f32[320]{0:T(512)S(1)}, f32[320]{0:T(512)}, u32[]{:S(2)}) copy-start(f32[320]{0:T(512)} %copy-done.187) | copy-start | bytes 3844
  1145.5 379.0 %reduce-scatter.17.cloned.1.call-start = ((), (), s32[]{:S(2)}) async-start(), calls=%async_computation.27 | async-start | bytes 10813440 | tf_op jit(solution)/shard_map/reduce_scatter | solution.py:105
  1147.4 81.9 %copy-start.84 = (f32[1056,640]{1,0:T(8,128)S(1)}, f32[1056,640]{1,0:T(8,128)}, u32[]{:S(2)}) copy-start(f32[1056,640]{1,0:T(8,128)} %copy.170) | copy-start | bytes 8110084
  1377.2 245.1 %reduce-scatter.29.cloned.1.call-start = ((), (), s32[]{:S(2)}) async-start(), calls=%async_computation.33 | async-start | bytes 14155776 | tf_op jit(solution)/shard_map/reduce_scatter | solution.py:263
  1391.0 327.6 %reduce-scatter.27.cloned.1.call-start = ((), (), s32[]{:S(2)}) async-start(), calls=%async_computation.32 | async-start | bytes 14155776 | tf_op jit(solution)/shard_map/reduce_scatter | solution.py:259
  1405.1 409.9 %reduce-scatter.25.cloned.1.call-start = ((), (), s32[]{:S(2)}) async-start(), calls=%async_computation.31 | async-start | bytes 14155776 | tf_op jit(solution)/shard_map/reduce_scatter | solution.py:258
  1418.9 446.6 %all-reduce.131.cloned.1.call-start = ((), (), s32[]{:S(2)}) async-start(), calls=%async_computation.34 | async-start | bytes 1310720 | tf_op jit(solution)/shard_map/psum | solution.py:265
  1424.2 501.9 %reduce-scatter.23.cloned.1.call-start = ((), (), s32[]{:S(2)}) async-start(), calls=%async_computation.30 | async-start | bytes 5898240 | tf_op jit(solution)/shard_map/reduce_scatter | solution.py:262
  1432.8 554.0 %reduce-scatter.21.cloned.1.call-start = ((), (), s32[]{:S(2)}) async-start(), calls=%async_computation.29 | async-start | bytes 5898240 | tf_op jit(solution)/shard_map/reduce_scatter | solution.py:257
  1442.9 604.5 %reduce-scatter.19.cloned.1.call-start = ((), (), s32[]{:S(2)}) async-start(), calls=%async_computation.28 | async-start | bytes 5898240 | tf_op jit(solution)/shard_map/reduce_scatter | solution.py:256
  (204 other events, 1933.9 us)
Sparse Core Ops, SparseCore 0:
  10.0 32.8 all-gather.14
  45.0 82.9 all-gather.10
  129.8 28.6 all-gather.12
  160.2 30.4 all-gather.16
  340.7 146.5 reduce-scatter.10
  489.0 46.3 all-gather.22
  537.6 82.9 all-gather.18
  622.4 44.0 all-gather.20
  668.6 82.9 all-gather.26
  753.3 45.1 all-gather.24
  840.0 148.5 reduce-scatter.14
  990.8 149.4 reduce-scatter.12
  1145.6 83.7 all-gather.28
  1377.3 147.1 reduce-scatter.16
  1528.4 93.7 reduce-scatter.28
  1626.1 92.3 reduce-scatter.26
  1722.5 92.3 reduce-scatter.24
  1818.4 47.0 all-reduce.130
  1869.4 56.5 reduce-scatter.22
  1930.2 56.5 reduce-scatter.20
  1990.8 56.5 reduce-scatter.18
where the time goes:
time: 2070 us; the launch traced here: 2060 us
  waiting for transfers between devices  1430 us (69%)
  matrix products  205 us (10%)
  local copies, waits for them, and re-layouts  191 us (9%)
  other arithmetic  132 us (6%)
  blocking collectives  77.9 us (4%)
    reduce_scatter x4, waiting for transfers between devices, collect_rows(): return lax.psum_scatter(values, 'rep', scatter_dimension=0, tiled=True)  484 us
    all_gather x4, waiting for transfers between devices, spread_rows(): return lax.all_gather(values, 'rep', axis=0, tiled=True)  320 us
    reduce_scatter x1, waiting for transfers between devices, body(): lax.psum_scatter(term_up, ('tok', 'blk'), scatter_dimension=0, tiled=True)  96.4 us
    reduce_scatter x1, waiting for transfers between devices, body(): lax.psum_scatter(term_gate, ('tok', 'blk'), scatter_dimension=0, tiled=True)  96.4 us
    dot_general x6, matrix products, transposed_times(): lax.dot_general(left_op, right_op, (((0,), (0,)), ((), ())), preferred_el...  67.7 us
    dot_general x6, matrix products, times_transposed(): lax.dot_general(left_op, right_op, (((1,), (1,)), ((), ())), preferred_el...  61.2 us
    reduce_scatter x1, waiting for transfers between devices, body(): lax.psum_scatter(term_branch, ('tok', 'blk'), scatter_dimension=0, tiled=...  60.8 us
    reduce_scatter x1, waiting for transfers between devices, body(): lax.psum_scatter(term_in, ('tok', 'blk'), scatter_dimension=0, tiled=True)  60.6 us
  transfers between devices with their start and end apart: 21, of which 19 were waited for; matrix products, arithmetic and copies ran while one was open for 16% of the time, Pallas kernels for 0%

commit v1 on v0

v1 whole, which is shorter than its diff:
```python
import jax
import jax.numpy as jnp
from jax import lax
from jax.experimental import pallas as pl
from jax.experimental.pallas import tpu as pltpu
from jax.sharding import PartitionSpec as P

SEQS = 2

epsilon = 1e-06
gate_power = 8.0
LANES = 128
SLAB = 8
STEP = 16
VMEM_BYTES = 56 * 1024 * 1024

f32 = jnp.float32
bf16 = jnp.bfloat16


def dot(left_op, right_op):
    return jnp.dot(left_op, right_op, preferred_element_type=f32)


def times_transposed(left_op, right_op):
    return lax.dot_general(left_op, right_op, (((1,), (1,)), ((), ())), preferred_element_type=f32)


def transposed_times(left_op, right_op):
    return lax.dot_general(left_op, right_op, (((0,), (0,)), ((), ())), preferred_element_type=f32)


def swap(values, axis, mask):
    size = lax.axis_size(axis)
    return lax.ppermute(values, axis, [(i, i ^ mask) for i in range(size)])


def in_order(first_is_mine, mine, other, axis):
    return jnp.concatenate(
        [jnp.where(first_is_mine, mine, other), jnp.where(first_is_mine, other, mine)], axis=axis
    )


def cut(values, start, size, axis=0):
    return lax.slice_in_dim(values, start, start + size, axis=axis)


def block_order(tok):
    if tok == 4:
        return [(0, 0), (0, 1), (1, 0), (3, 0), (2, 1), (3, 1), (1, 1), (2, 0)]
    return [(j, h) for j in range(tok) for h in range(2)]


def flip_blocks(blocks, tok):
    index = lax.axis_index("tok")
    bit = 1
    while bit < tok:
        flipped = (index & bit) != 0
        blocks = [jnp.where(flipped, blocks[k ^ (2 * bit)], blocks[k]) for k in range(len(blocks))]
        bit *= 2
    return blocks


def to_own_order(values):
    tok = lax.axis_size("tok")
    width = values.shape[-1] // (2 * tok)
    blocks = [cut(values, k * width, width, values.ndim - 1) for k in range(2 * tok)]
    blocks = flip_blocks(blocks, tok)
    return jnp.concatenate([blocks[2 * j + h] for j, h in block_order(tok)], axis=-1)


def from_own_order(values):
    tok = lax.axis_size("tok")
    width = values.shape[-1] // (2 * tok)
    blocks = [None] * (2 * tok)
    for place, (j, h) in enumerate(block_order(tok)):
        blocks[2 * j + h] = cut(values, place * width, width, values.ndim - 1)
    return jnp.concatenate(flip_blocks(blocks, tok), axis=-1)


def gather_pieces(piece, axis):
    tok = lax.axis_size("tok")
    if tok != 4:
        return [piece] + [swap(piece, "tok", j) for j in range(1, tok)]
    half = piece.shape[axis] // 2
    from_x = swap(piece, "tok", 1)
    from_y = swap(piece, "tok", 2)
    far_a = swap(cut(from_x, 0, half, axis), "tok", 2)
    far_b = swap(cut(from_y, half, half, axis), "tok", 1)
    return [
        piece,
        cut(from_x, 0, half, axis),
        far_a,
        cut(from_y, half, half, axis),
        far_b,
        cut(from_x, half, half, axis),
        cut(from_y, 0, half, axis),
    ]


def scatter_pieces(make, extent, axis):
    tok = lax.axis_size("tok")
    if tok != 4:
        size = extent // tok
        total = make(0, size)
        for j in range(1, tok):
            total = total + swap(make(j * size, size).astype(bf16), "tok", j).astype(f32)
        return total
    w = extent // 8
    from_x = swap(make(2 * w, 2 * w).astype(bf16), "tok", 1)
    from_y = swap(make(4 * w, 2 * w).astype(bf16), "tok", 2)
    rest = make(6 * w, 2 * w)
    own = make(0, 2 * w)
    onward_x = cut(rest, 0, w, axis) + cut(from_y, w, w, axis).astype(f32)
    onward_y = cut(rest, w, w, axis) + cut(from_x, w, w, axis).astype(f32)
    last_b = swap(onward_x.astype(bf16), "tok", 1).astype(f32)
    last_a = swap(onward_y.astype(bf16), "tok", 2).astype(f32)
    return own + jnp.concatenate(
        [cut(from_x, 0, w, axis).astype(f32) + last_a, cut(from_y, 0, w, axis).astype(f32) + last_b],
        axis=axis,
    )


def gather_rows(values):
    core = lax.axis_index("blk")
    low = (lax.axis_index("rep") & 1) == 0
    half = in_order(low, values, swap(values, "rep", 1), 0)
    return in_order(core == 0, half, swap(half, "blk", 1), 0)


def reduce_rows(make, rows):
    core = lax.axis_index("blk")
    low = lax.axis_index("rep") & 1
    other = make((1 - core) * (2 * rows), 2 * rows).astype(bf16)
    from_core = swap(other, "blk", 1)
    mine = make(core * (2 * rows), 2 * rows) + from_core.astype(f32)
    send = lax.dynamic_slice_in_dim(mine, (1 - low) * rows, rows).astype(bf16)
    keep = lax.dynamic_slice_in_dim(mine, low * rows, rows)
    return keep + swap(send, "rep", 1).astype(f32)


def row_range(values):
    return lambda start, size: lax.dynamic_slice_in_dim(values, start, size)


def normalize(values, gain_vec):
    inverse = lax.rsqrt(jnp.mean(values * values, axis=-1, keepdims=True) + epsilon)
    scaled = values * inverse
    return (scaled * gain_vec, scaled, inverse)


def normalize_back(grad_in, gain_vec, scaled, inverse):
    weighted = grad_in * gain_vec
    through = inverse * (weighted - scaled * jnp.mean(weighted * scaled, axis=-1, keepdims=True))
    return (through, jnp.sum(grad_in * scaled, axis=0))


def row_iota():
    return lax.broadcasted_iota(jnp.int32, (SLAB, LANES), 0)


def since_start(info, run, row):
    slot = row_iota() + (info[2 + run] + row)
    begin = jnp.where(slot >= info[1], info[1], jnp.where(slot >= info[0], info[0], 0))
    return slot - begin


def down(before, now, k):
    return jnp.where(row_iota() < k, pltpu.roll(before, k, 0), pltpu.roll(now, k, 0))


def up(now, after, k):
    return jnp.where(row_iota() < SLAB - k, pltpu.roll(now, SLAB - k, 0), pltpu.roll(after, SLAB - k, 0))


def last_row(values):
    return jnp.broadcast_to(values[SLAB - 1 : SLAB, :], (SLAB, LANES))


def first_row(values):
    return jnp.broadcast_to(values[0:1, :], (SLAB, LANES))


def scan_slab(rates, pushes, reverse):
    for d in (1, 2, 4):
        shift = SLAB - d if reverse else d
        mask = row_iota() < SLAB - d if reverse else row_iota() >= d
        far_rate = pltpu.roll(rates, shift, 0)
        far_push = pltpu.roll(pushes, shift, 0)
        pushes = jnp.where(mask, rates * far_push + pushes, pushes)
        rates = jnp.where(mask, rates * far_rate, rates)
    return rates, pushes


def chunks(channels):
    return [pl.ds(c * LANES, LANES) for c in range(channels // LANES)]


def row(params_ref, index, c):
    return params_ref[index : index + 1, c]


def forward_kernel(run_rows, info, x_ref, halo_ref, gates_ref, params_ref,
                   conv_ref, low_ref, r_ref, g_ref, a_ref, local_ref, reach_ref, ends_ref, mixed_ref):
    rows, channels = x_ref.shape
    steps = run_rows // STEP

    for run in range(2):
        base = run * run_rows

        def conv_step(i, before, base=base, run=run):
            at = pl.multiple_of(base + i * STEP, STEP)
            far = [since_start(info, run, i * STEP + s * SLAB) for s in range(2)]
            after = []
            for n, c in enumerate(chunks(channels)):
                x = x_ref[pl.ds(at, STEP), c].astype(f32)
                prev = before[n]
                outs = []
                for s in range(2):
                    now = x[s * SLAB : (s + 1) * SLAB]
                    total = row(params_ref, 4, c) + row(params_ref, 0, c) * now
                    for k in (1, 2, 3):
                        total = total + row(params_ref, k, c) * jnp.where(far[s] >= k, down(prev, now, k), 0.0)
                    outs.append(total)
                    prev = now
                both = jnp.concatenate(outs, axis=0)
                conv_ref[pl.ds(at, STEP), c] = both
                low_ref[pl.ds(at, STEP), c] = both.astype(bf16)
                after.append(prev)
            return tuple(after)

        first = tuple(halo_ref[run, :, c] for c in chunks(channels))
        lax.fori_loop(0, steps, conv_step, first)

    tile = rows // 6
    def gate_step(i, _):
        at = pl.multiple_of(i * tile, STEP)
        mixed_ref[pl.ds(at, tile), :] = jnp.dot(low_ref[pl.ds(at, tile), :], gates_ref[...], preferred_element_type=f32)
        return 0
    lax.fori_loop(0, 6, gate_step, 0)

    for run in range(2):
        base = run * run_rows

        def scan_step(i, carried, base=base, run=run):
            at = pl.multiple_of(base + i * STEP, STEP)
            far = [since_start(info, run, i * STEP + s * SLAB) for s in range(2)]
            after = []
            for n, c in enumerate(chunks(channels)):
                state, reach = carried[n]
                second = pl.ds(channels + n * LANES, LANES)
                for s in range(2):
                    here = pl.ds(pl.multiple_of(at + s * SLAB, SLAB), SLAB)
                    r = jax.nn.sigmoid(mixed_ref[here, c] + row(params_ref, 5, c))
                    g = jax.nn.sigmoid(mixed_ref[here, second] + row(params_ref, 6, c))
                    log_a = row(params_ref, 7, c) * r
                    e = jnp.exp(log_a)
                    power = jnp.maximum(-jnp.tanh(log_a) * (1.0 + e * e), 0.0)
                    a = jnp.where(far[s] >= 1, e, 0.0)
                    r_ref[here, c] = r
                    g_ref[here, c] = g
                    a_ref[here, c] = a
                    rates, pushes = scan_slab(a, jnp.sqrt(power) * g * conv_ref[here, c], False)
                    local_ref[here, c] = pushes + rates * state
                    reach_ref[here, c] = rates * reach
                    state = last_row(pushes) + last_row(rates) * state
                    reach = last_row(rates) * reach
                after.append((state, reach))
            return tuple(after)

        zero = tuple((jnp.zeros((SLAB, LANES), f32), jnp.ones((SLAB, LANES), f32)) for _ in chunks(channels))
        done = lax.fori_loop(0, steps, scan_step, zero)
        for n, c in enumerate(chunks(channels)):
            ends_ref[run, :, c] = done[n][0]
            ends_ref[2 + run, :, c] = done[n][1]


def backward_scan_kernel(run_rows, a_ref, grad_ref, part_ref, reach_ref, ends_ref):
    channels = a_ref.shape[1]
    steps = run_rows // STEP
    for run in range(2):
        base = run * run_rows

        def step(j, carried, base=base):
            at = pl.multiple_of(base + (steps - 1 - j) * STEP, STEP)
            after = []
            for n, c in enumerate(chunks(channels)):
                flow, reach = carried[n]
                grads = grad_ref[pl.ds(at, STEP), c].astype(f32)
                for s in (1, 0):
                    here = pl.ds(pl.multiple_of(at + s * SLAB, SLAB), SLAB)
                    grad = grads[s * SLAB : (s + 1) * SLAB]
                    a = a_ref[here, c]
                    rates, pushes = scan_slab(a, a * grad, True)
                    flows = pushes + rates * flow
                    reaches = rates * reach
                    part_ref[here, c] = grad + up(flows, flow, 1)
                    reach_ref[here, c] = up(reaches, reach, 1)
                    flow = first_row(pushes) + first_row(rates) * flow
                    reach = first_row(rates) * reach
                after.append((flow, reach))
            return tuple(after)

        zero = tuple((jnp.zeros((SLAB, LANES), f32), jnp.ones((SLAB, LANES), f32)) for _ in chunks(channels))
        done = lax.fori_loop(0, steps, step, zero)
        for n, c in enumerate(chunks(channels)):
            ends_ref[run, :, c] = done[n][0]


def backward_kernel(run_rows, info, part_ref, reach_ref, flow_ref, states_ref, enter_ref, r_ref, g_ref, conv_ref,
                    gates_ref, params_ref, mixed_ref, conv_grad_ref, sums_ref):
    rows, channels = r_ref.shape
    steps = run_rows // STEP
    sums_ref[...] = jnp.zeros(sums_ref.shape, f32)
    for run in range(2):
        base = run * run_rows

        def step(i, carried, base=base, run=run):
            at = pl.multiple_of(base + i * STEP, STEP)
            far = [since_start(info, run, i * STEP + s * SLAB) for s in range(2)]
            after = []
            for n, c in enumerate(chunks(channels)):
                prev, sum_a, sum_i, sum_d = carried[n]
                second = pl.ds(channels + n * LANES, LANES)
                flow = flow_ref[run, :, c]
                grads_a, grads_i = [], []
                for s in range(2):
                    here = pl.ds(pl.multiple_of(at + s * SLAB, SLAB), SLAB)
                    total = part_ref[here, c] + reach_ref[here, c] * flow
                    states = states_ref[here, c]
                    r, g, conv = r_ref[here, c], g_ref[here, c], conv_ref[here, c]
                    log_a = row(params_ref, 7, c) * r
                    e = jnp.exp(log_a)
                    power = jnp.maximum(-jnp.tanh(log_a) * (1.0 + e * e), 0.0)
                    inverse = lax.rsqrt(power)
                    root = power * inverse
                    a = jnp.where(far[s] >= 1, e, 0.0)
                    through = total * g
                    grad_log = total * down(prev, states, 1) * a - through * conv * (e * e) * inverse
                    grad_a = grad_log * row(params_ref, 7, c) * r * (1.0 - r)
                    direct = through * root
                    grad_i = direct * conv * (1.0 - g)
                    conv_grad_ref[here, c] = direct
                    sum_a = sum_a + grad_a
                    sum_i = sum_i + grad_i
                    sum_d = sum_d + grad_log * r
                    grads_a.append(grad_a)
                    grads_i.append(grad_i)
                    prev = states
                mixed_ref[pl.ds(at, STEP), c] = jnp.concatenate(grads_a, axis=0).astype(bf16)
                mixed_ref[pl.ds(at, STEP), second] = jnp.concatenate(grads_i, axis=0).astype(bf16)
                after.append((prev, sum_a, sum_i, sum_d))
            return tuple(after)

        nothing = jnp.zeros((SLAB, LANES), f32)
        first = tuple((enter_ref[run, :, c], nothing, nothing, nothing) for c in chunks(channels))
        done = lax.fori_loop(0, steps, step, first)
        for n, c in enumerate(chunks(channels)):
            for k in range(3):
                sums_ref[k : k + 1, c] += jnp.sum(done[n][1 + k], axis=0, keepdims=True)

    tile = rows // 6
    def gate_step(i, _):
        at = pl.multiple_of(i * tile, STEP)
        conv_grad_ref[pl.ds(at, tile), :] += times_transposed(mixed_ref[pl.ds(at, tile), :], gates_ref[...])
        return 0
    lax.fori_loop(0, 6, gate_step, 0)


def conv_back_kernel(run_rows, info, conv_grad_ref, halo_ref, x_ref, params_ref, grad_ref, sums_ref):
    rows, channels = x_ref.shape
    steps = run_rows // STEP
    sums_ref[...] = jnp.zeros(sums_ref.shape, f32)
    for run in range(2):
        base = run * run_rows

        def step(j, carried, base=base, run=run):
            i = steps - 1 - j
            at = pl.multiple_of(base + i * STEP, STEP)
            far = [since_start(info, run, i * STEP + s * SLAB) for s in range(3)]
            after = []
            for n, c in enumerate(chunks(channels)):
                later, totals = carried[n]
                totals = list(totals)
                x = x_ref[pl.ds(at, STEP), c].astype(f32)
                outs = [None, None]
                for s in (1, 0):
                    now = conv_grad_ref[pl.ds(pl.multiple_of(at + s * SLAB, SLAB), SLAB), c]
                    here = x[s * SLAB : (s + 1) * SLAB]
                    out = row(params_ref, 0, c) * now
                    totals[0] = totals[0] + now * here
                    for k in (1, 2, 3):
                        moved = up(jnp.where(far[s] >= k, now, 0.0), jnp.where(far[s + 1] >= k, later, 0.0), k)
                        out = out + row(params_ref, k, c) * moved
                        totals[k] = totals[k] + moved * here
                    totals[4] = totals[4] + now
                    outs[s] = out
                    later = now
                grad_ref[pl.ds(at, STEP), c] = jnp.concatenate(outs, axis=0).astype(bf16)
                after.append((later, tuple(totals)))
            return tuple(after)

        nothing = jnp.zeros((SLAB, LANES), f32)
        first = tuple((halo_ref[run, :, c], (nothing,) * 5) for c in chunks(channels))
        done = lax.fori_loop(0, steps, step, first)
        for n, c in enumerate(chunks(channels)):
            for k in range(5):
                sums_ref[k : k + 1, c] += jnp.sum(done[n][1][k], axis=0, keepdims=True)


def call_kernel(kernel, inputs, outputs, flops=0, scratch=(), scalars=True):
    vmem = pl.BlockSpec(memory_space=pltpu.VMEM)
    smem = pl.BlockSpec(memory_space=pltpu.SMEM)
    specs = [smem if scalars and k == 0 else vmem for k in range(len(inputs))]
    moved = sum(v.size * v.dtype.itemsize for v in inputs) + sum(
        o[0][0] * o[0][1] * jnp.dtype(o[1]).itemsize for o in outputs
    )
    return pl.pallas_call(
        kernel,
        in_specs=specs,
        out_specs=[vmem] * len(outputs),
        out_shape=[jax.ShapeDtypeStruct(s, d) for s, d in outputs],
        scratch_shapes=list(scratch),
        compiler_params=pltpu.CompilerParams(vmem_limit_bytes=VMEM_BYTES),
        cost_estimate=pl.CostEstimate(flops=flops, bytes_accessed=moved, transcendentals=0),
    )(*inputs)


def body(
    block_input,
    cotangent,
    segment_ids,
    norm_gain,
    mlp_gain,
    w_input,
    w_branch,
    w_output,
    w_gate,
    w_up,
    w_down,
    gate_a,
    gate_i,
    conv_weight,
    conv_bias,
    bias_a,
    bias_i,
    decay_param,
):
    rows, width = block_input.shape
    bucket = segment_ids.shape[0]
    core = lax.axis_index("blk")
    rep = lax.axis_index("rep")
    first_core = core == 0
    early = (rep & 2) == 0

    run_rows = 2 * rows
    group_rows = 2 * run_rows
    taps = conv_weight.shape[0]
    own_channels = conv_weight.shape[-1]
    channels = 2 * own_channels
    blocks = gate_a.shape[2]
    block_width = gate_a.shape[3]
    own_hidden = w_gate.shape[1] // 2
    hidden_count = 2 * own_hidden

    start1 = jnp.sum((segment_ids < 1).astype(jnp.int32))
    start2 = jnp.sum((segment_ids < 2).astype(jnp.int32))
    run_base = (rep // 2) * run_rows
    info = jnp.stack([start1, start2, run_base, run_base + bucket // 2]).astype(jnp.int32)
    own_slot = core * (bucket // 2) + rep * rows + jnp.arange(rows, dtype=jnp.int32)
    valid = (own_slot < start2).astype(f32)[:, None]

    gain1 = to_own_order(norm_gain[None, :])
    gain2 = to_own_order(mlp_gain[None, :])

    x_first = to_own_order(block_input).astype(f32)
    normed1, scaled1, inverse1 = normalize(x_first, gain1)
    rows1 = gather_rows(normed1.astype(bf16))

    def split_columns(values):
        half = values.shape[1] // 2
        low, high = values[:, :half], values[:, half:]
        return jnp.where(first_core, low, high), jnp.where(first_core, high, low)

    def split_rows(values):
        half = values.shape[0] // 2
        low, high = values[:half], values[half:]
        return jnp.where(first_core, low, high), jnp.where(first_core, high, low)

    def row_weights(one, two):
        one_mine, one_other = split_columns(one)
        two_mine, two_other = split_columns(two)
        mine = jnp.concatenate([one_mine, two_mine], axis=1)
        came = swap(jnp.concatenate([one_other, two_other], axis=1), "blk", 1)
        own = in_order(first_core, mine, came, 0)
        far = swap(own, "rep", 2)
        n = one_mine.shape[1]
        piece = jnp.concatenate([own[:, :n], far[:, :n], own[:, n:], far[:, n:]], axis=1)
        pieces = gather_pieces(piece, 0)
        return (
            jnp.concatenate([p[:, : 2 * n] for p in pieces], axis=0),
            jnp.concatenate([p[:, 2 * n :] for p in pieces], axis=0),
        )

    def column_weights(values):
        mine, other = split_rows(values)
        came = swap(other, "blk", 1)
        own = in_order(first_core, mine, came, 1)
        piece = jnp.concatenate([own, swap(own, "rep", 2)], axis=0)
        return jnp.concatenate(gather_pieces(piece, 1), axis=1)

    full_in, full_branch = row_weights(w_input, w_branch)

    small = jnp.concatenate(
        [
            conv_weight.reshape(taps, own_channels),
            conv_bias.reshape(1, own_channels),
            bias_a.reshape(1, own_channels),
            bias_i.reshape(1, own_channels),
            decay_param.reshape(1, own_channels),
        ],
        axis=0,
    )
    small = jnp.concatenate([small, swap(small, "rep", 2)], axis=1)
    decay_row = small[taps + 3 :]
    params = jnp.concatenate([small[: taps + 3], -gate_power * jax.nn.softplus(-decay_row)], axis=0)
    gates = jnp.stack(
        [gate_a.reshape(blocks, block_width, block_width), gate_i.reshape(blocks, block_width, block_width)]
    )
    gates = jnp.concatenate([gates, swap(gates, "rep", 2)], axis=1)

    def spread_gate(gate):
        strips = []
        for k in range(2 * blocks):
            left = jnp.zeros((block_width, k * block_width), bf16)
            right = jnp.zeros((block_width, (2 * blocks - 1 - k) * block_width), bf16)
            strips.append(jnp.concatenate([left, gate[k], right], axis=1))
        return jnp.concatenate(strips, axis=0)

    gate_matrix = jnp.concatenate([spread_gate(gates[0]), spread_gate(gates[1])], axis=1)

    def from_far(values):
        came = swap(values, "rep", 2)
        return jnp.concatenate([came[..., own_channels:], came[..., :own_channels]], axis=-1)

    mixer_in = dot(rows1, full_in).astype(bf16)
    branch = dot(rows1, full_branch)
    tails = jnp.stack([mixer_in[run_rows - SLAB : run_rows], mixer_in[group_rows - SLAB :]])
    tails = from_far(tails).astype(f32)
    halo = jnp.stack([tails[0], jnp.where(early, tails[0], tails[1])])
    full = (group_rows, channels)
    conv_out, conv_low, gate_r, gate_in, decays, local, reach, ends = call_kernel(
        lambda *refs: forward_kernel(run_rows, *refs),
        (info, mixer_in, halo, gate_matrix, params),
        ((full, f32), (full, bf16), (full, f32), (full, f32), (full, f32), (full, f32), (full, f32),
         ((4, SLAB, channels), f32)),
        flops=4 * group_rows * channels * channels,
        scratch=(pltpu.VMEM((group_rows, 2 * channels), f32),),
    )
    own_end = ends[:, 0]
    far_end = from_far(own_end)
    h0, h1, p0, p1 = own_end[0], own_end[1], own_end[2], own_end[3]
    fh0, fh1, fp0, fp1 = far_end[0], far_end[1], far_end[2], far_end[3]
    enter0 = jnp.where(early, jnp.zeros_like(fh0), fh0)
    enter1 = jnp.where(early, fh0 + fp0 * h0, fh1 + fp1 * (h0 + p0 * fh0))
    enter = jnp.stack([enter0, enter1])
    states = (
        local.reshape(2, run_rows, channels) + reach.reshape(2, run_rows, channels) * enter[:, None, :]
    ).reshape(full)
    states_low = states.astype(bf16).astype(f32)
    activated = jax.nn.gelu(branch)
    merged = (activated * states_low).astype(bf16)

    full_out = column_weights(w_output)
    take_merged = row_range(merged)
    residual = x_first + reduce_rows(lambda s, n: dot(take_merged(s, n), full_out), rows)

    normed2, scaled2, inverse2 = normalize(residual, gain2)
    rows2 = gather_rows(normed2.astype(bf16))
    full_gate, full_up = row_weights(w_gate, w_up)
    gate_pre = dot(rows2, full_gate)
    up_pre = dot(rows2, full_up)
    gate_act, gate_back = jax.vjp(jax.nn.gelu, gate_pre)
    hidden = (gate_act * up_pre).astype(bf16)
    full_down = column_weights(w_down)

    grad_final = to_own_order(cotangent).astype(f32) * valid
    final_grad_rows = gather_rows(grad_final.astype(bf16))
    grad_hidden = times_transposed(final_grad_rows, full_down)
    grad_gate = gate_back(grad_hidden * up_pre)[0].astype(bf16)
    grad_up = (grad_hidden * gate_act).astype(bf16)
    take_gate, take_up = row_range(grad_gate), row_range(grad_up)
    grad_normed2 = reduce_rows(
        lambda s, n: times_transposed(take_gate(s, n), full_gate) + times_transposed(take_up(s, n), full_up), rows
    )
    through2, gain2_term = normalize_back(grad_normed2, gain2, scaled2, inverse2)
    grad_residual = grad_final + through2
    residual_rows = gather_rows(grad_residual.astype(bf16))

    take_hidden = row_range(hidden)
    final_rows = residual + reduce_rows(lambda s, n: dot(take_hidden(s, n), full_down), rows)
    block_out = from_own_order(final_rows.astype(bf16))

    def own_columns(values, axis):
        half = values.shape[axis] // 2
        return [cut(values, k * half, half, axis) for k in range(2)]

    def finish_rows(total, n):
        far = jnp.concatenate([total[:, n : 2 * n], total[:, 3 * n :]], axis=1).astype(bf16)
        own = jnp.concatenate([total[:, :n], total[:, 2 * n : 3 * n]], axis=1) + swap(far, "rep", 2).astype(f32)
        low, high = own_columns(own, 0)
        mine = jnp.where(first_core, low, high)
        came = swap(jnp.where(first_core, high, low), "blk", 1)
        return tuple(in_order(first_core, cut(mine, k * n, n, 1), cut(came, k * n, n, 1), 1) for k in range(2))

    def finish_columns(total):
        n = total.shape[0] // 2
        own = total[:n] + swap(total[n:].astype(bf16), "rep", 2).astype(f32)
        low, high = own_columns(own, 1)
        mine = jnp.where(first_core, low, high)
        came = swap(jnp.where(first_core, high, low), "blk", 1)
        return in_order(first_core, mine, came, 0)

    down_total = scatter_pieces(
        lambda s, n: transposed_times(hidden, cut(final_grad_rows, s, n, 1)), width, 1
    )
    grad_down_w = finish_columns(down_total)
    both_grads = jnp.concatenate([grad_gate, grad_up], axis=1)
    mlp_total = scatter_pieces(lambda s, n: transposed_times(cut(rows2, s, n, 1), both_grads), width, 0)
    grad_gate_w, grad_up_w = finish_rows(mlp_total, own_hidden)

    grad_merged = times_transposed(residual_rows, full_out)
    _, branch_back = jax.vjp(jax.nn.gelu, branch)
    grad_branch = branch_back(grad_merged * states_low)[0].astype(bf16)
    grad_states = (grad_merged * activated).astype(bf16)
    part, back_reach, flows = call_kernel(
        lambda *refs: backward_scan_kernel(run_rows, *refs),
        (decays, grad_states),
        ((full, f32), (full, f32), ((2, SLAB, channels), f32)),
        scalars=False,
    )
    own_flow = flows[:, 0]
    far_flow = from_far(own_flow)
    u0, u1 = own_flow[0], own_flow[1]
    fu0, fu1 = far_flow[0], far_flow[1]
    flow1 = jnp.where(early, fu1, jnp.zeros_like(fu1))
    flow0 = jnp.where(early, fu0 + fp0 * (u1 + p1 * fu1), fu1 + fp1 * u1)

    def wide(values):
        return jnp.broadcast_to(values[:, None, :], (2, SLAB, channels))

    grad_mixed, grad_conv, sums = call_kernel(
        lambda *refs: backward_kernel(run_rows, *refs),
        (info, part, back_reach, wide(jnp.stack([flow0, flow1])), states, wide(enter), gate_r, gate_in, conv_out,
         gate_matrix, params),
        (((group_rows, 2 * channels), bf16), (full, f32), ((SLAB, channels), f32)),
        flops=4 * group_rows * channels * channels,
    )
    heads = from_far(jnp.stack([grad_conv[:SLAB], grad_conv[run_rows : run_rows + SLAB]]))
    after = jnp.stack(
        [jnp.where(early, heads[0], heads[1]), jnp.where(early, heads[1], jnp.zeros_like(heads[1]))]
    )
    grad_mixer_in, conv_sums = call_kernel(
        lambda *refs: conv_back_kernel(run_rows, *refs),
        (info, grad_conv, after, mixer_in, params),
        ((full, bf16), ((SLAB, channels), f32)),
    )
    take_in, take_branch = row_range(grad_mixer_in), row_range(grad_branch)
    grad_normed1 = reduce_rows(
        lambda s, n: times_transposed(take_in(s, n), full_in) + times_transposed(take_branch(s, n), full_branch),
        rows,
    )
    through1, gain1_term = normalize_back(grad_normed1, gain1, scaled1, inverse1)
    input_grad = from_own_order(grad_residual + through1)

    out_total = scatter_pieces(
        lambda s, n: transposed_times(merged, cut(residual_rows, s, n, 1)), width, 1
    )
    grad_out_w = finish_columns(out_total)
    mixer_grads = jnp.concatenate([grad_mixer_in, grad_branch], axis=1)
    mixer_total = scatter_pieces(lambda s, n: transposed_times(cut(rows1, s, n, 1), mixer_grads), width, 0)
    grad_in_w, grad_branch_w = finish_rows(mixer_total, own_channels)

    def sum_over(values, axis):
        size = lax.axis_size(axis)
        bit = 1
        while bit < size:
            values = values + swap(values, axis, bit)
            bit *= 2
        return values

    gate_grads = transposed_times(conv_low, grad_mixed)

    def gate_block(which, k):
        at = k * block_width
        return gate_grads[at : at + block_width, which * channels + at : which * channels + at + block_width]

    own_gates = jnp.stack([jnp.stack([gate_block(w, k) for k in range(blocks)]) for w in range(2)])
    far_gates = jnp.stack([jnp.stack([gate_block(w, k) for k in range(blocks, 2 * blocks)]) for w in range(2)])
    gate_sum = sum_over(own_gates + swap(far_gates, "rep", 2), "tok")
    decay_grad = sums[2:3] * (gate_power * jax.nn.sigmoid(-decay_row))
    small_grads = jnp.concatenate([conv_sums[: taps + 1], sums[:2], decay_grad], axis=0)
    small_sum = sum_over(small_grads[:, :own_channels] + swap(small_grads[:, own_channels:], "rep", 2), "tok")

    gain_terms = from_own_order(jnp.stack([gain1_term, gain2_term]))
    gain_sum = sum_over(sum_over(sum_over(gain_terms, "blk"), "rep"), "tok")

    return (
        block_out,
        input_grad,
        gain_sum[0],
        gain_sum[1],
        grad_in_w,
        grad_branch_w,
        grad_out_w,
        grad_gate_w,
        grad_up_w,
        grad_down_w,
        gate_sum[0].reshape(gate_a.shape),
        gate_sum[1].reshape(gate_i.shape),
        small_sum[:taps].reshape(conv_weight.shape),
        small_sum[taps].reshape(conv_bias.shape),
        small_sum[taps + 1].reshape(bias_a.shape),
        small_sum[taps + 2].reshape(bias_i.shape),
        small_sum[taps + 3].reshape(decay_param.shape),
    )


def solution(mesh):
    rows_spec = P(("tok", "blk", "rep"), None)
    by_rows = P(("tok", "blk"), "rep")
    by_columns = P("rep", ("tok", "blk"))
    channel = P("rep", "blk", None)
    gate_spec = P("rep", "blk", None, None, None)
    taps_spec = P(None, "rep", "blk", None)
    return jax.shard_map(
        body,
        mesh=mesh,
        in_specs=(
            rows_spec, rows_spec, P("tok"), P(), P(),
            by_rows, by_rows, by_columns, by_rows, by_rows, by_columns,
            gate_spec, gate_spec, taps_spec, channel, channel, channel, channel,
        ),
        out_specs=(
            rows_spec, rows_spec, P(), P(),
            by_rows, by_rows, by_columns, by_rows, by_rows, by_columns,
            gate_spec, gate_spec, taps_spec, channel, channel, channel, channel,
        ),
        check_vma=False,
    )
```

time: 2070 us -> 1080 us (0.52)
  waiting for transfers between devices: 1430 us -> 568 us
  local copies, waits for them, and re-layouts: 191 us -> 58.4 us
  blocking collectives: 77.9 us -> 0 us
  starting transfers between devices: 1.11 us -> 73.7 us
  Pallas kernels: 0 us -> 53.1 us
  matrix products: 205 us -> 184 us
    reduce_scatter x10 -> x0, waiting for transfers between devices: 909 us -> none  [the longest x4 484 us: collect_rows(): return lax.psum_scatter(values, 'rep', scatter_dimension=0, tiled=True)]
    ppermute x0 -> x81, waiting for transfers between devices: none -> 568 us  [swap(): return lax.ppermute(values, axis, [(i, i ^ mask) for i in range(size)])]
    all_gather x10 -> x0, waiting for transfers between devices: 470 us -> none  [the longest x4 320 us: spread_rows(): return lax.all_gather(values, 'rep', axis=0, tiled=True)]
    ppermute x0 -> x81, starting transfers between devices: none -> 73.7 us  [swap(): return lax.ppermute(values, axis, [(i, i ^ mask) for i in range(size)])]
    psum x2 -> x0, blocking collectives: 58 us -> none  [the longest x1 41.5 us: body(): lax.psum((gain1_term, gain2_term), ('tok', 'blk', 'rep'))]
    pallas_call x0 -> x4, Pallas kernels: none -> 53.1 us  [call_kernel(): pl.pallas_call(kernel, in_specs=specs, out_specs=[vmem] * len(outputs), o...]
    psum x1 -> x0, waiting for transfers between devices: 50.5 us -> none  [body(): lax.psum((grad_gate_a.reshape(gate_a.shape), grad_gate_i.reshape(gate_i.s...]
    slice x55 -> x23, local copies, waits for them, and re-layouts: 63.8 us -> 13.5 us  [the longest x8 7.32 us: cut(): return lax.slice_in_dim(values, start, start + size, axis=axis)]
  transfers between devices with their start and end apart: 21 -> 81, of which waited for: 19 -> 34; matrix products, arithmetic and copies ran while one was open for 16% -> 26% of each run, Pallas kernels for 0% -> 5%
where the time goes in v1:
time: 1080 us; the launch traced here: 1070 us
  waiting for transfers between devices  568 us (53%)
  matrix products  184 us (17%)
  other arithmetic  127 us (12%)
  starting transfers between devices  73.7 us (7%)
  local copies, waits for them, and re-layouts  58.4 us (5%)
  Pallas kernels  53.1 us (5%)
    ppermute x81, waiting for transfers between devices, swap(): return lax.ppermute(values, axis, [(i, i ^ mask) for i in range(size)])  568 us
    ppermute x81, starting transfers between devices, swap(): return lax.ppermute(values, axis, [(i, i ^ mask) for i in range(size)])  73.7 us
    dot_general x17, matrix products, transposed_times(): lax.dot_general(left_op, right_op, (((0,), (0,)), ((), ())), preferred_el...  68.7 us
    dot_general x10, matrix products, times_transposed(): lax.dot_general(left_op, right_op, (((1,), (1,)), ((), ())), preferred_el...  61.9 us
    dot_general x8, matrix products, dot(): return jnp.dot(left_op, right_op, preferred_element_type=f32)  53.3 us
    pallas_call x4, Pallas kernels, call_kernel(): pl.pallas_call(kernel, in_specs=specs, out_specs=[vmem] * len(outputs), o...  53.1 us
    unnamed x258, local copies, waits for them, and re-layouts  24.7 us
  transfers between devices with their start and end apart: 81, of which 34 were waited for; matrix products, arithmetic and copies ran while one was open for 26% of the time, Pallas kernels for 5%

profile of v1, /device:TPU:0, one launch (start us, length us, event | category | flops | bytes accessed | tf_op | source)
XLA Modules:
  0.0 1067.3 jit_solution(1143613358194436869)
XLA Ops:
  29.7 10.6 collective-permute-done.10
  49.3 17.3 %fusion.48.refs_3_.refs_9_ = bf16[640,1280]{1,0:T(8,128)(2,1)} fusion(bf16[160,160]{1,0:T(8,128)(2,1)S(1)} %get-tuple-element.207, bf16[160,160]{1,0:T(8,128)(2,1)S(1)} %copy-done.67, bf16[160,160]{1,0:T(8,128)(2,1)S(1)} %get-tuple-element.209, bf16[160,160]{1,0:T(8,128)(2,1)S(1)} %copy-done.68, bf16[160,160]{1,0:T(8,128)(2,1)S(1)} %broadcast.113, ...), kind=kLoop, calls=%fused_computation.161 | loop fusion | flops 39321600 | bytes 2201600 | tf_op jit(solution)/shard_map/concatenate | solution.py:540
  72.9 26.4 %collective-permute-done.13 = bf16[320,512]{1,0:T(8,128)(2,1)S(1)} collective-permute-done((bf16[320,512]{1,0:T(8,128)(2,1)S(1)}, bf16[320,512]{1,0:T(8,128)(2,1)S(1)}, u32[]{:S(2)}, u32[]{:S(2)}) %collective-permute-start.13) | collective-permute-done | bytes 327712 | tf_op jit(solution)/shard_map/ppermute | solution.py:35
  104.7 25.4 %collective-permute-done.3 = bf16[512,640]{1,0:T(8,128)(2,1)S(1)} collective-permute-done((bf16[512,640]{1,0:T(8,128)(2,1)S(1)}, bf16[512,640]{1,0:T(8,128)(2,1)S(1)}, u32[]{:S(2)}, u32[]{:S(2)}) %collective-permute-start.3) | collective-permute-done | bytes 655392 | tf_op jit(solution)/shard_map/ppermute | solution.py:35
  132.6 4.2 concatenate.227
  146.6 5.0 collective-permute-done.15
  157.3 23.4 %collective-permute-done.29 = bf16[768,512]{1,0:T(8,128)(2,1)} collective-permute-done((bf16[768,512]{1,0:T(8,128)(2,1)}, bf16[768,512]{1,0:T(8,128)(2,1)}, u32[]{:S(2)}, u32[]{:S(2)}) %collective-permute-start.29) | collective-permute-done | bytes 786464 | tf_op jit(solution)/shard_map/ppermute | solution.py:35
  195.6 17.5 %collective-permute-done.23 = bf16[512,1536]{1,0:T(8,128)(2,1)S(1)} collective-permute-done((bf16[512,1536]{1,0:T(8,128)(2,1)S(1)}, bf16[512,1536]{1,0:T(8,128)(2,1)S(1)}, u32[]{:S(2)}, u32[]{:S(2)}) %collective-permute-start.23) | collective-permute-done | bytes 1572896 | tf_op jit(solution)/shard_map/ppermute | solution.py:35
  217.6 27.2 %collective-permute-done.7 = bf16[256,1280]{1,0:T(8,128)(2,1)S(1)} collective-permute-done((bf16[256,1280]{1,0:T(8,128)(2,1)S(1)}, bf16[256,1280]{1,0:T(8,128)(2,1)S(1)}, u32[]{:S(2)}, u32[]{:S(2)}) %collective-permute-start.7) | collective-permute-done | bytes 655392 | tf_op jit(solution)/shard_map/ppermute | solution.py:35
  256.6 20.4 %shard_map.305 = (f32[1056,640]{1,0:T(8,128)}, bf16[1056,640]{1,0:T(8,128)(2,1)}, f32[1056,640]{1,0:T(8,128)}, f32[1056,640]{1,0:T(8,128)}, f32[1056,640]{1,0:T(...) custom-call(s32[4]{0:T(128)} %pad_add_fusion.refs_0_, bf16[1056,640]{1,0:T(8,128)(2,1)} %copy-done.50, ...), custom_call_target="tpu_custom_call" | custom-call | flops 1730150400 | bytes 20623504 | tf_op jit(solution)/shard_map/pallas_call | solution.py:418
  279.9 5.4 fusion.29
  307.2 72.3 %collective-permute-done.33 = bf16[1536,256]{1,0:T(8,128)(2,1)S(1)} collective-permute-done((bf16[1536,256]{1,0:T(8,128)(2,1)S(1)}, bf16[1536,256]{1,0:T(8,128)(2,1)S(1)}, u32[]{:S(2)}, u32[]{:S(2)}) %collective-permute-start.33) | collective-permute-done | bytes 786464 | tf_op jit(solution)/shard_map/ppermute | solution.py:35
  385.4 11.2 %fusion.8 = f32[1056,1536]{1,0:T(8,128)} fusion(bf16[1536,2048]{1,0:T(8,128)(2,1)} %slice_dynamic-update-slice_fusion, bf16[528,2048]{1,0:T(8,128)(2,1)S(1)} %get-tuple-element.96, bf16[528,2048]{1,0:T(8,128)(2,1)S(1)} %get-tuple-element.95), kind=kOutput, calls=%fused_computation.53 | convolution fusion | flops 6652428288 | bytes 17104896 | tf_op jit(solution)/shard_map/dot_general | solution.py:26
  399.6 10.6 collective-permute-done.20
  411.2 8.3 collective-permute-done.25
  422.1 10.1 collective-permute-done.27
  440.2 9.8 fusion.27
  450.0 19.0 %fusion.6 = (bf16[1056,1536]{1,0:T(8,128)(2,1)}, bf16[1056,1536]{1,0:T(8,128)(2,1)}, bf16[1056,1536]{1,0:T(8,128)(2,1)}) fusion(f32[1056,1536]{1,0:T(8,128)} %fusion.8, f32[1056,1536]{1,0:T(8,128)} %fusion.27, bf16[2048,1536]{1,0:T(8,128)(2,1)} %get-tuple-element.119, bf16[528,2048]{1,0:T(8,128)(2,1)S(1)} %get-tuple-element.98, ...), kind=kOutput, calls=%fused_computation.44 | convolution fusion | flops 6694600704 | bytes 33325056 | tf_op jit(solution)/shard_map/dot_general | solution.py:22
  469.0 6.3 fusion.57
  475.3 8.1 fusion.54
  483.4 4.9 convolution_convert_fusion.4
  497.5 9.1 convolution_convert_fusion
  506.7 8.4 convolution_convert_fusion.1
  518.1 6.9 add_convert_fusion.1
  525.5 7.6 fusion.91
  533.1 6.2 fusion.59
  539.3 12.8 %collective-permute-done.69 = bf16[1536,512]{1,0:T(8,128)(2,1)S(1)} collective-permute-done((bf16[1536,512]{1,0:T(8,128)(2,1)}, bf16[1536,512]{1,0:T(8,128)(2,1)S(1)}, u32[]{:S(2)}, u32[]{:S(2)}) %collective-permute-start.69) | collective-permute-done | bytes 1572896 | tf_op jit(solution)/shard_map/ppermute | solution.py:35
  556.6 6.9 convert_add_fusion.2
  564.9 72.6 %collective-permute-done.70 = bf16[1536,256]{1,0:T(8,128)(2,1)S(1)} collective-permute-done((bf16[1536,256]{1,0:T(8,128)(2,1)S(1)}, bf16[1536,256]{1,0:T(8,128)(2,1)S(1)}, u32[]{:S(2)}, u32[]{:S(2)}) %collective-permute-start.70) | collective-permute-done | bytes 786464 | tf_op jit(solution)/shard_map/ppermute | solution.py:35
  648.4 32.0 %collective-permute-done.73 = bf16[768,512]{1,0:T(8,128)(2,1)S(1)} collective-permute-done((bf16[768,512]{1,0:T(8,128)(2,1)S(1)}, bf16[768,512]{1,0:T(8,128)(2,1)S(1)}, u32[]{:S(2)}, u32[]{:S(2)}) %collective-permute-start.73) | collective-permute-done | bytes 786464 | tf_op jit(solution)/shard_map/ppermute | solution.py:35
  683.2 5.1 fusion.26
  690.3 12.5 %collective-permute-done.39 = bf16[264,2048]{1,0:T(8,128)(2,1)S(1)} collective-permute-done((bf16[264,2048]{1,0:T(8,128)(2,1)S(1)}, bf16[264,2048]{1,0:T(8,128)(2,1)S(1)}, u32[]{:S(2)}, u32[]{:S(2)}) %collective-permute-start.39) | collective-permute-done | bytes 1081376 | tf_op jit(solution)/shard_map/ppermute | solution.py:35
  708.3 16.2 %collective-permute-done.64 = bf16[256,3072]{1,0:T(8,128)(2,1)} collective-permute-done((bf16[256,3072]{1,0:T(8,128)(2,1)}, bf16[256,3072]{1,0:T(8,128)(2,1)}, u32[]{:S(2)}, u32[]{:S(2)}) %collective-permute-start.64) | collective-permute-done | bytes 1572896 | tf_op jit(solution)/shard_map/ppermute | solution.py:35
  730.1 11.0 %fusion.196 = (bf16[512,3072]{1,0:T(8,128)(2,1)}, f32[512,3072]{1,0:T(8,128)}) fusion(f32[256,3072]{1,0:T(8,128)S(1)} %convert_add_fusion.5, f32[256,3072]{1,0:T(8,128)S(1)} %convert_add_fusion.6, bf16[1056,1536]{1,0:T(8,128)(2,1)} %get-tuple-element.85, bf16[1056,1536]{1,0:T(8,128)(2,1)} %get-tuple-element.84, bf16[528,2048]{1,0:T(8,128)(2,1)S(1)} %copy-done.40, ...), kind=kOutput, calls=%fused_computation.646 | convolution fusion | flops 3341746176 | bytes 26542080 | tf_op jit(solution)/shard_map/dot_general | solution.py:30
  751.8 61.2 %collective-permute-done.67 = bf16[512,1536]{1,0:T(8,128)(2,1)S(1)} collective-permute-done((bf16[512,1536]{1,0:T(8,128)(2,1)S(1)}, bf16[512,1536]{1,0:T(8,128)(2,1)S(1)}, u32[]{:S(2)}, u32[]{:S(2)}) %collective-permute-start.67) | collective-permute-done | bytes 1572896 | tf_op jit(solution)/shard_map/ppermute | solution.py:35
  821.6 7.7 multiply_convert_fusion.2
  835.1 8.7 shard_map.306
  852.7 16.9 %shard_map.307 = (bf16[1056,1280]{1,0:T(8,128)(2,1)}, f32[1056,640]{1,0:T(8,128)}, f32[8,640]{1,0:T(8,128)}) custom-call(s32[4]{0:T(128)} %pad_add_fusion.refs_0_, f32[1056,640]{1,0:T(8,128)} %get-tuple-element.37.refs_1_, f32[1056,640]{1,0:T(8,128)} %get-tuple-element.38.refs_2_, f32[2,8,640]{2,1,0:T(8,128)} %broadcast_in_dim.12.refs_3_, ...), custom_call_target="tpu_custom_call" | custom-call | flops 1730150400 | bytes 23388176 | tf_op jit(solution)/shard_map/pallas_call | solution.py:418
  873.3 4.5 fusion.197
  882.9 7.0 shard_map.308
  897.7 5.7 add_convert_fusion
  905.4 4.1 collective-permute-done.78
  923.7 37.4 %collective-permute-done.76 = f32[2,2,160,160]{3,2,1,0:T(8,128)S(1)} collective-permute-done((f32[2,2,160,160]{3,2,1,0:T(8,128)S(1)}, f32[2,2,160,160]{3,2,1,0:T(8,128)S(1)}, u32[]{:S(2)}, u32[]{:S(2)}) %collective-permute-start.76) | collective-permute-done | bytes 409632 | tf_op jit(solution)/shard_map/ppermute | solution.py:35
  972.2 5.0 collective-permute-done.77
  978.2 7.3 collective-permute-done.61
  991.3 12.5 %collective-permute-done.52 = bf16[256,1280]{1,0:T(8,128)(2,1)S(1)} collective-permute-done((bf16[256,1280]{1,0:T(8,128)(2,1)S(1)}, bf16[256,1280]{1,0:T(8,128)(2,1)S(1)}, u32[]{:S(2)}, u32[]{:S(2)}) %collective-permute-start.52) | collective-permute-done | bytes 655392 | tf_op jit(solution)/shard_map/ppermute | solution.py:35
  1012.3 24.8 %collective-permute-done.55 = bf16[512,640]{1,0:T(8,128)(2,1)S(1)} collective-permute-done((bf16[512,640]{1,0:T(8,128)(2,1)S(1)}, bf16[512,640]{1,0:T(8,128)(2,1)S(1)}, u32[]{:S(2)}, u32[]{:S(2)}) %collective-permute-start.55) | collective-permute-done | bytes 655392 | tf_op jit(solution)/shard_map/ppermute | solution.py:35
  1037.6 10.3 collective-permute-done.45
  (640 shorter events, 300.0 us)
Async XLA Ops:
  6.6 131.8 %collective-permute-start = (bf16[264,2048]{1,0:T(8,128)(2,1)}, bf16[264,2048]{1,0:T(8,128)(2,1)}, u32[]{:S(2)}, u32[]{:S(2)}) collective-permute-start(bf16[264,2048]{1,0:T(8,128)(2,1)} %fusion.39), channel_id=1, source_target_pairs={{0,1},{1,0},{2,3},{3,2},{4,5},{5,4},{6,7},{7,6},{8,9},{9,8},{10,11... | collective-permute-start | bytes 3244040 | tf_op jit(solution)/shard_map/ppermute | solution.py:35
  11.3 55.3 %collective-permute-start.2 = (bf16[256,640]{1,0:T(8,128)(2,1)}, bf16[256,640]{1,0:T(8,128)(2,1)}, u32[]{:S(2)}, u32[]{:S(2)}) collective-permute-start(bf16[256,640]{1,0:T(8,128)(2,1)} %pad_maximum_fusion.36), channel_id=1, source_target_pairs={{0,4},{4,0},{1,5},{5,1},{2,6},{6,2},{3,7},{7,3},{8,12},{12,8},{9,1... | collective-permute-start | bytes 983048 | tf_op jit(solution)/shard_map/ppermute | solution.py:35
  40.2 60.2 %collective-permute-start.22 = (bf16[256,1536]{1,0:T(8,128)(2,1)}, bf16[256,1536]{1,0:T(8,128)(2,1)S(1)}, u32[]{:S(2)}, u32[]{:S(2)}) collective-permute-start(bf16[256,1536]{1,0:T(8,128)(2,1)} %pad_maximum_fusion.26), channel_id=1, source_target_pairs={{0,4},{4,0},{1,5},{5,1},{2,6},{6,2},{3,7},{7,3},{8,12},{12,8},{9,1... | collective-permute-start | bytes 2359304 | tf_op jit(solution)/shard_map/ppermute | solution.py:35
  44.6 99.4 %collective-permute-start.36 = (bf16[264,2048]{1,0:T(8,128)(2,1)}, bf16[264,2048]{1,0:T(8,128)(2,1)}, u32[]{:S(2)}, u32[]{:S(2)}) collective-permute-start(bf16[264,2048]{1,0:T(8,128)(2,1)} %fusion.46), channel_id=1, source_target_pairs={{0,1},{1,0},{2,3},{3,2},{4,5},{5,4},{6,7},{7,6},{8,9},{9,8},{10,11... | collective-permute-start | bytes 3244040 | tf_op jit(solution)/shard_map/ppermute | solution.py:35
  66.6 32.6 %collective-permute-start.13 = (bf16[320,512]{1,0:T(8,128)(2,1)S(1)}, bf16[320,512]{1,0:T(8,128)(2,1)S(1)}, u32[]{:S(2)}, u32[]{:S(2)}) collective-permute-start(bf16[320,512]{1,0:T(8,128)(2,1)S(1)} %pad_maximum_fusion.38), channel_id=1, source_target_pairs={{0,2},{1,3},{2,0},{3,1},{4,6},{5,7},{6,4},{7,5},{8,10},{9,11},{10,... | collective-permute-start | bytes 983048 | tf_op jit(solution)/shard_map/ppermute | solution.py:35
  68.2 61.9 %collective-permute-start.3 = (bf16[512,640]{1,0:T(8,128)(2,1)S(1)}, bf16[512,640]{1,0:T(8,128)(2,1)S(1)}, u32[]{:S(2)}, u32[]{:S(2)}) collective-permute-start(bf16[512,640]{1,0:T(8,128)(2,1)S(1)} %pad_maximum_fusion.24), channel_id=1, source_target_pairs={{0,2},{1,3},{2,0},{3,1},{4,6},{5,7},{6,4},{7,5},{8,10},{9,11},{10,... | collective-permute-start | bytes 1966088 | tf_op jit(solution)/shard_map/ppermute | solution.py:35
  99.2 81.6 %collective-permute-start.29 = (bf16[768,512]{1,0:T(8,128)(2,1)}, bf16[768,512]{1,0:T(8,128)(2,1)}, u32[]{:S(2)}, u32[]{:S(2)}) collective-permute-start(bf16[768,512]{1,0:T(8,128)(2,1)} %pad_maximum_fusion.27), channel_id=1, source_target_pairs={{0,2},{1,3},{2,0},{3,1},{4,6},{5,7},{6,4},{7,5},{8,10},{9,11},{10,... | collective-permute-start | bytes 2359304 | tf_op jit(solution)/shard_map/ppermute | solution.py:35
  100.4 40.1 %collective-permute-start.14 = (bf16[640,512]{1,0:T(8,128)(2,1)}, bf16[640,512]{1,0:T(8,128)(2,1)}, u32[]{:S(2)}, u32[]{:S(2)}) collective-permute-start(bf16[640,512]{1,0:T(8,128)(2,1)} %get-tuple-element.214), channel_id=1, source_target_pairs={{0,8},{8,0},{16,24},{24,16},{1,9},{9,1},{17,25},{25,17},{2,10},{10... | collective-permute-start | bytes 1966088 | tf_op jit(solution)/shard_map/ppermute | solution.py:35
  138.4 74.7 %collective-permute-start.23 = (bf16[512,1536]{1,0:T(8,128)(2,1)S(1)}, bf16[512,1536]{1,0:T(8,128)(2,1)S(1)}, u32[]{:S(2)}, u32[]{:S(2)}) collective-permute-start(bf16[512,1536]{1,0:T(8,128)(2,1)S(1)} %copy-done.46), channel_id=1, source_target_pairs={{0,2},{1,3},{2,0},{3,1},{4,6},{5,7},{6,4},{7,5},{8,10},{9,11},{10,... | collective-permute-start | bytes 4718600 | tf_op jit(solution)/shard_map/ppermute | solution.py:35
  140.6 50.0 %collective-permute-start.4 = (bf16[512,1280]{1,0:T(8,128)(2,1)S(1)}, bf16[512,1280]{1,0:T(8,128)(2,1)S(1)}, u32[]{:S(2)}, u32[]{:S(2)}) collective-permute-start(bf16[512,1280]{1,0:T(8,128)(2,1)S(1)} %copy-done.59), channel_id=1, source_target_pairs={{0,8},{8,0},{16,24},{24,16},{1,9},{9,1},{17,25},{25,17},{2,10},{10... | collective-permute-start | bytes 3932168 | tf_op jit(solution)/shard_map/ppermute | solution.py:35
  151.6 42.4 %collective-permute-start.6 = (bf16[512,1280]{1,0:T(8,128)(2,1)S(1)}, bf16[512,1280]{1,0:T(8,128)(2,1)S(1)}, u32[]{:S(2)}, u32[]{:S(2)}) collective-permute-start(bf16[512,1280]{1,0:T(8,128)(2,1)S(1)} %copy-done.59), channel_id=1, source_target_pairs={{0,16},{8,24},{16,0},{24,8},{1,17},{9,25},{17,1},{25,9},{2,18},{10... | collective-permute-start | bytes 3932168 | tf_op jit(solution)/shard_map/ppermute | solution.py:35
  155.6 89.5 %collective-permute-start.1 = (bf16[528,2048]{1,0:T(8,128)(2,1)S(1)}, bf16[528,2048]{1,0:T(8,128)(2,1)S(1)}, u32[]{:S(2)}, u32[]{:S(2)}) collective-permute-start(bf16[528,2048]{1,0:T(8,128)(2,1)S(1)} %pad_maximum_fusion.13), channel_id=1, source_target_pairs={{0,4},{4,0},{1,5},{5,1},{2,6},{6,2},{3,7},{7,3},{8,12},{12,8},{9,1... | collective-permute-start | bytes 6488072 | tf_op jit(solution)/shard_map/ppermute | solution.py:35
  188.1 113.8 %collective-permute-start.37 = (bf16[528,2048]{1,0:T(8,128)(2,1)}, bf16[528,2048]{1,0:T(8,128)(2,1)}, u32[]{:S(2)}, u32[]{:S(2)}) collective-permute-start(bf16[528,2048]{1,0:T(8,128)(2,1)} %pad_maximum_fusion.15), channel_id=1, source_target_pairs={{0,4},{4,0},{1,5},{5,1},{2,6},{6,2},{3,7},{7,3},{8,12},{12,8},{9,1... | collective-permute-start | bytes 6488072 | tf_op jit(solution)/shard_map/ppermute | solution.py:35
  194.0 57.1 %collective-permute-start.30 = (bf16[1536,512]{1,0:T(8,128)(2,1)}, bf16[1536,512]{1,0:T(8,128)(2,1)S(1)}, u32[]{:S(2)}, u32[]{:S(2)}) collective-permute-start(bf16[1536,512]{1,0:T(8,128)(2,1)} %get-tuple-element.186), channel_id=1, source_target_pairs={{0,8},{8,0},{16,24},{24,16},{1,9},{9,1},{17,25},{25,17},{2,10},{10... | collective-permute-start | bytes 4718600 | tf_op jit(solution)/shard_map/ppermute | solution.py:35
  215.9 83.2 %collective-permute-start.32 = (bf16[1536,512]{1,0:T(8,128)(2,1)}, bf16[1536,512]{1,0:T(8,128)(2,1)}, u32[]{:S(2)}, u32[]{:S(2)}) collective-permute-start(bf16[1536,512]{1,0:T(8,128)(2,1)} %get-tuple-element.186), channel_id=1, source_target_pairs={{0,16},{8,24},{16,0},{24,8},{1,17},{9,25},{17,1},{25,9},{2,18},{10... | collective-permute-start | bytes 4718600 | tf_op jit(solution)/shard_map/ppermute | solution.py:35
  252.5 44.0 %collective-permute-start.31 = (bf16[1536,256]{1,0:T(8,128)(2,1)}, bf16[1536,256]{1,0:T(8,128)(2,1)}, u32[]{:S(2)}, u32[]{:S(2)}) collective-permute-start(bf16[1536,256]{1,0:T(8,128)(2,1)} %get-tuple-element.156), channel_id=1, source_target_pairs={{0,16},{8,24},{16,0},{24,8},{1,17},{9,25},{17,1},{25,9},{2,18},{10... | collective-permute-start | bytes 2359304 | tf_op jit(solution)/shard_map/ppermute | solution.py:35
  292.4 91.3 %collective-permute-start.24 = (bf16[512,3072]{1,0:T(8,128)(2,1)S(1)}, bf16[512,3072]{1,0:T(8,128)(2,1)S(1)}, u32[]{:S(2)}, u32[]{:S(2)}) collective-permute-start(bf16[512,3072]{1,0:T(8,128)(2,1)S(1)} %pad_maximum_fusion.7), channel_id=1, source_target_pairs={{0,8},{8,0},{16,24},{24,16},{1,9},{9,1},{17,25},{25,17},{2,10},{10... | collective-permute-start | bytes 9437192 | tf_op jit(solution)/shard_map/ppermute | solution.py:35
  296.5 100.1 %collective-permute-start.26 = (bf16[512,3072]{1,0:T(8,128)(2,1)S(1)}, bf16[512,3072]{1,0:T(8,128)(2,1)S(1)}, u32[]{:S(2)}, u32[]{:S(2)}) collective-permute-start(bf16[512,3072]{1,0:T(8,128)(2,1)S(1)} %pad_maximum_fusion.7), channel_id=1, source_target_pairs={{0,16},{8,24},{16,0},{24,8},{1,17},{9,25},{17,1},{25,9},{2,18},{10... | collective-permute-start | bytes 9437192 | tf_op jit(solution)/shard_map/ppermute | solution.py:35
  301.3 78.2 %collective-permute-start.33 = (bf16[1536,256]{1,0:T(8,128)(2,1)S(1)}, bf16[1536,256]{1,0:T(8,128)(2,1)S(1)}, u32[]{:S(2)}, u32[]{:S(2)}) collective-permute-start(bf16[1536,256]{1,0:T(8,128)(2,1)S(1)} %get-tuple-element.154), channel_id=1, source_target_pairs={{0,8},{8,0},{16,24},{24,16},{1,9},{9,1},{17,25},{25,17},{2,10},{10... | collective-permute-start | bytes 2359304 | tf_op jit(solution)/shard_map/ppermute | solution.py:35
  307.1 77.3 %collective-permute-start.19 = (bf16[264,2048]{1,0:T(8,128)(2,1)S(1)}, bf16[264,2048]{1,0:T(8,128)(2,1)S(1)}, u32[]{:S(2)}, u32[]{:S(2)}) collective-permute-start(bf16[264,2048]{1,0:T(8,128)(2,1)S(1)} %dynamic-slice_convert_fusion.3), channel_id=1, source_target_pairs={{0,1},{1,0},{2,3},{3,2},{4,5},{5,4},{6,7},{7,6},{8,9},{9,8},{10,11... | collective-permute-start | bytes 3244040 | tf_op jit(solution)/shard_map/ppermute | solution.py:35
  383.8 35.8 %collective-permute-start.25 = (bf16[256,3072]{1,0:T(8,128)(2,1)S(1)}, bf16[256,3072]{1,0:T(8,128)(2,1)S(1)}, u32[]{:S(2)}, u32[]{:S(2)}) collective-permute-start(bf16[256,3072]{1,0:T(8,128)(2,1)S(1)} %slice.1114), channel_id=1, source_target_pairs={{0,16},{8,24},{16,0},{24,8},{1,17},{9,25},{17,1},{25,9},{2,18},{10... | collective-permute-start | bytes 4718600 | tf_op jit(solution)/shard_map/ppermute | solution.py:35
  396.7 35.5 %collective-permute-start.27 = (bf16[256,3072]{1,0:T(8,128)(2,1)S(1)}, bf16[256,3072]{1,0:T(8,128)(2,1)S(1)}, u32[]{:S(2)}, u32[]{:S(2)}) collective-permute-start(bf16[256,3072]{1,0:T(8,128)(2,1)S(1)} %slice.1117), channel_id=1, source_target_pairs={{0,8},{8,0},{16,24},{24,16},{1,9},{9,1},{17,25},{25,17},{2,10},{10... | collective-permute-start | bytes 4718600 | tf_op jit(solution)/shard_map/ppermute | solution.py:35
  515.0 41.1 %collective-permute-start.34 = (bf16[528,2048]{1,0:T(8,128)(2,1)}, bf16[528,2048]{1,0:T(8,128)(2,1)}, u32[]{:S(2)}, u32[]{:S(2)}) collective-permute-start(bf16[528,2048]{1,0:T(8,128)(2,1)} %convolution_convert_fusion.4), channel_id=1, source_target_pairs={{0,4},{4,0},{1,5},{5,1},{2,6},{6,2},{3,7},{7,3},{8,12},{12,8},{9,1... | collective-permute-start | bytes 6488072 | tf_op jit(solution)/shard_map/ppermute | solution.py:35
  515.0 37.0 %collective-permute-start.69 = (bf16[1536,512]{1,0:T(8,128)(2,1)}, bf16[1536,512]{1,0:T(8,128)(2,1)S(1)}, u32[]{:S(2)}, u32[]{:S(2)}) collective-permute-start(bf16[1536,512]{1,0:T(8,128)(2,1)} %convolution_convert_fusion.6), channel_id=1, source_target_pairs={{0,8},{8,0},{16,24},{24,16},{1,9},{9,1},{17,25},{25,17},{2,10},{10... | collective-permute-start | bytes 4718600 | tf_op jit(solution)/shard_map/ppermute | solution.py:35
  516.6 37.5 %collective-permute-start.71 = (bf16[1536,512]{1,0:T(8,128)(2,1)}, bf16[1536,512]{1,0:T(8,128)(2,1)S(1)}, u32[]{:S(2)}, u32[]{:S(2)}) collective-permute-start(bf16[1536,512]{1,0:T(8,128)(2,1)} %convolution_convert_fusion.5), channel_id=1, source_target_pairs={{0,16},{8,24},{16,0},{24,8},{1,17},{9,25},{17,1},{25,9},{2,18},{10... | collective-permute-start | bytes 4718600 | tf_op jit(solution)/shard_map/ppermute | solution.py:35
  525.0 119.8 %collective-permute-start.38 = (bf16[528,2048]{1,0:T(8,128)(2,1)}, bf16[528,2048]{1,0:T(8,128)(2,1)}, u32[]{:S(2)}, u32[]{:S(2)}) collective-permute-start(bf16[528,2048]{1,0:T(8,128)(2,1)} %add_convert_fusion.1), channel_id=1, source_target_pairs={{0,4},{4,0},{1,5},{5,1},{2,6},{6,2},{3,7},{7,3},{8,12},{12,8},{9,1... | collective-permute-start | bytes 6488072 | tf_op jit(solution)/shard_map/ppermute | solution.py:35
  525.0 158.2 %collective-permute-start.65 = (bf16[512,3072]{1,0:T(8,128)(2,1)}, bf16[512,3072]{1,0:T(8,128)(2,1)}, u32[]{:S(2)}, u32[]{:S(2)}) collective-permute-start(bf16[512,3072]{1,0:T(8,128)(2,1)} %convolution_convert_fusion), channel_id=1, source_target_pairs={{0,16},{8,24},{16,0},{24,8},{1,17},{9,25},{17,1},{25,9},{2,18},{10... | collective-permute-start | bytes 9437192 | tf_op jit(solution)/shard_map/ppermute | solution.py:35
  552.0 131.1 %collective-permute-start.63 = (bf16[512,3072]{1,0:T(8,128)(2,1)}, bf16[512,3072]{1,0:T(8,128)(2,1)}, u32[]{:S(2)}, u32[]{:S(2)}) collective-permute-start(bf16[512,3072]{1,0:T(8,128)(2,1)} %convolution_convert_fusion.1), channel_id=1, source_target_pairs={{0,8},{8,0},{16,24},{24,16},{1,9},{9,1},{17,25},{25,17},{2,10},{10... | collective-permute-start | bytes 9437192 | tf_op jit(solution)/shard_map/ppermute | solution.py:35
  554.5 83.0 %collective-permute-start.70 = (bf16[1536,256]{1,0:T(8,128)(2,1)S(1)}, bf16[1536,256]{1,0:T(8,128)(2,1)S(1)}, u32[]{:S(2)}, u32[]{:S(2)}) collective-permute-start(bf16[1536,256]{1,0:T(8,128)(2,1)S(1)} %get-tuple-element.109), channel_id=1, source_target_pairs={{0,16},{8,24},{16,0},{24,8},{1,17},{9,25},{17,1},{25,9},{2,18},{10... | collective-permute-start | bytes 2359304 | tf_op jit(solution)/shard_map/ppermute | solution.py:35
  556.1 83.1 %collective-permute-start.72 = (bf16[1536,256]{1,0:T(8,128)(2,1)S(1)}, bf16[1536,256]{1,0:T(8,128)(2,1)S(1)}, u32[]{:S(2)}, u32[]{:S(2)}) collective-permute-start(bf16[1536,256]{1,0:T(8,128)(2,1)S(1)} %get-tuple-element.110), channel_id=1, source_target_pairs={{0,8},{8,0},{16,24},{24,16},{1,9},{9,1},{17,25},{25,17},{2,10},{10... | collective-permute-start | bytes 2359304 | tf_op jit(solution)/shard_map/ppermute | solution.py:35
  637.5 66.2 %collective-permute-start.35 = (bf16[264,2048]{1,0:T(8,128)(2,1)}, bf16[264,2048]{1,0:T(8,128)(2,1)}, u32[]{:S(2)}, u32[]{:S(2)}) collective-permute-start(bf16[264,2048]{1,0:T(8,128)(2,1)} %dynamic-slice_convert_fusion.2), channel_id=1, source_target_pairs={{0,1},{1,0},{2,3},{3,2},{4,5},{5,4},{6,7},{7,6},{8,9},{9,8},{10,11... | collective-permute-start | bytes 3244040 | tf_op jit(solution)/shard_map/ppermute | solution.py:35
  643.3 37.1 %collective-permute-start.73 = (bf16[768,512]{1,0:T(8,128)(2,1)S(1)}, bf16[768,512]{1,0:T(8,128)(2,1)S(1)}, u32[]{:S(2)}, u32[]{:S(2)}) collective-permute-start(bf16[768,512]{1,0:T(8,128)(2,1)S(1)} %slice.2326), channel_id=1, source_target_pairs={{0,2},{1,3},{2,0},{3,1},{4,6},{5,7},{6,4},{7,5},{8,10},{9,11},{10,... | collective-permute-start | bytes 2359304 | tf_op jit(solution)/shard_map/ppermute | solution.py:35
  647.9 55.0 %collective-permute-start.39 = (bf16[264,2048]{1,0:T(8,128)(2,1)S(1)}, bf16[264,2048]{1,0:T(8,128)(2,1)S(1)}, u32[]{:S(2)}, u32[]{:S(2)}) collective-permute-start(bf16[264,2048]{1,0:T(8,128)(2,1)S(1)} %dynamic-slice_convert_fusion.1), channel_id=1, source_target_pairs={{0,1},{1,0},{2,3},{3,2},{4,5},{5,4},{6,7},{7,6},{8,9},{9,8},{10,11... | collective-permute-start | bytes 3244040 | tf_op jit(solution)/shard_map/ppermute | solution.py:35
  683.1 65.6 %collective-permute-start.74 = (f32[768,256]{1,0:T(8,128)}, f32[768,256]{1,0:T(8,128)}, u32[]{:S(2)}, u32[]{:S(2)}) collective-permute-start(f32[768,256]{1,0:T(8,128)} %slice_select_fusion.2), channel_id=1, source_target_pairs={{0,4},{4,0},{1,5},{5,1},{2,6},{6,2},{3,7},{7,3},{8,12},{12,8},{9,1... | collective-permute-start | bytes 2359304 | tf_op jit(solution)/shard_map/ppermute | solution.py:35
  688.3 36.2 %collective-permute-start.64 = (bf16[256,3072]{1,0:T(8,128)(2,1)}, bf16[256,3072]{1,0:T(8,128)(2,1)}, u32[]{:S(2)}, u32[]{:S(2)}) collective-permute-start(bf16[256,3072]{1,0:T(8,128)(2,1)} %get-tuple-element.89), channel_id=1, source_target_pairs={{0,16},{8,24},{16,0},{24,8},{1,17},{9,25},{17,1},{25,9},{2,18},{10... | collective-permute-start | bytes 4718600 | tf_op jit(solution)/shard_map/ppermute | solution.py:35
  689.8 37.1 %collective-permute-start.66 = (bf16[256,3072]{1,0:T(8,128)(2,1)S(1)}, bf16[256,3072]{1,0:T(8,128)(2,1)}, u32[]{:S(2)}, u32[]{:S(2)}) collective-permute-start(bf16[256,3072]{1,0:T(8,128)(2,1)S(1)} %get-tuple-element.90), channel_id=1, source_target_pairs={{0,8},{8,0},{16,24},{24,16},{1,9},{9,1},{17,25},{25,17},{2,10},{10... | collective-permute-start | bytes 4718600 | tf_op jit(solution)/shard_map/ppermute | solution.py:35
  706.1 40.0 %collective-permute-start.40 = (bf16[264,2048]{1,0:T(8,128)(2,1)S(1)}, bf16[264,2048]{1,0:T(8,128)(2,1)}, u32[]{:S(2)}, u32[]{:S(2)}) collective-permute-start(bf16[264,2048]{1,0:T(8,128)(2,1)S(1)} %get-tuple-element.74), channel_id=1, source_target_pairs={{0,1},{1,0},{2,3},{3,2},{4,5},{5,4},{6,7},{7,6},{8,9},{9,8},{10,11... | collective-permute-start | bytes 3244040 | tf_op jit(solution)/shard_map/ppermute | solution.py:35
  742.7 70.4 %collective-permute-start.67 = (bf16[512,1536]{1,0:T(8,128)(2,1)S(1)}, bf16[512,1536]{1,0:T(8,128)(2,1)S(1)}, u32[]{:S(2)}, u32[]{:S(2)}) collective-permute-start(bf16[512,1536]{1,0:T(8,128)(2,1)S(1)} %pad_maximum_fusion.20), channel_id=1, source_target_pairs={{0,2},{1,3},{2,0},{3,1},{4,6},{5,7},{6,4},{7,5},{8,10},{9,11},{10,... | collective-permute-start | bytes 4718600 | tf_op jit(solution)/shard_map/ppermute | solution.py:35
  747.9 67.1 %collective-permute-start.41 = (bf16[528,2048]{1,0:T(8,128)(2,1)S(1)}, bf16[528,2048]{1,0:T(8,128)(2,1)S(1)}, u32[]{:S(2)}, u32[]{:S(2)}) collective-permute-start(bf16[528,2048]{1,0:T(8,128)(2,1)S(1)} %pad_maximum_fusion.16), channel_id=1, source_target_pairs={{0,4},{4,0},{1,5},{5,1},{2,6},{6,2},{3,7},{7,3},{8,12},{12,8},{9,1... | collective-permute-start | bytes 6488072 | tf_op jit(solution)/shard_map/ppermute | solution.py:35
  815.0 172.0 %collective-permute-start.68 = (f32[256,1536]{1,0:T(8,128)}, f32[256,1536]{1,0:T(8,128)}, u32[]{:S(2)}, u32[]{:S(2)}) collective-permute-start(f32[256,1536]{1,0:T(8,128)} %get-tuple-element.116), channel_id=1, source_target_pairs={{0,4},{4,0},{1,5},{5,1},{2,6},{6,2},{3,7},{7,3},{8,12},{12,8},{9,1... | collective-permute-start | bytes 4718600 | tf_op jit(solution)/shard_map/ppermute | solution.py:35
  848.5 71.7 %collective-permute-start.59 = (bf16[640,512]{1,0:T(8,128)(2,1)}, bf16[640,512]{1,0:T(8,128)(2,1)}, u32[]{:S(2)}, u32[]{:S(2)}) collective-permute-start(bf16[640,512]{1,0:T(8,128)(2,1)} %convolution_convert_fusion.9), channel_id=1, source_target_pairs={{0,16},{8,24},{16,0},{24,8},{1,17},{9,25},{17,1},{25,9},{2,18},{10... | collective-permute-start | bytes 1966088 | tf_op jit(solution)/shard_map/ppermute | solution.py:35
  850.0 70.8 %collective-permute-start.57 = (bf16[640,512]{1,0:T(8,128)(2,1)}, bf16[640,512]{1,0:T(8,128)(2,1)}, u32[]{:S(2)}, u32[]{:S(2)}) collective-permute-start(bf16[640,512]{1,0:T(8,128)(2,1)} %convolution_convert_fusion.10), channel_id=1, source_target_pairs={{0,8},{8,0},{16,24},{24,16},{1,9},{9,1},{17,25},{25,17},{2,10},{10... | collective-permute-start | bytes 1966088 | tf_op jit(solution)/shard_map/ppermute | solution.py:35
  879.1 38.4 %collective-permute-start.75 = (f32[2,2,160,160]{3,2,1,0:T(8,128)}, f32[2,2,160,160]{3,2,1,0:T(8,128)}, u32[]{:S(2)}, u32[]{:S(2)}) collective-permute-start(f32[2,2,160,160]{3,2,1,0:T(8,128)} %pad_maximum_fusion.34), channel_id=1, source_target_pairs={{0,2},{1,3},{2,0},{3,1},{4,6},{5,7},{6,4},{7,5},{8,10},{9,11},{10,... | collective-permute-start | bytes 1228808 | tf_op jit(solution)/shard_map/ppermute | solution.py:35
  917.0 69.4 %collective-permute-start.53 = (bf16[512,1280]{1,0:T(8,128)(2,1)S(1)}, bf16[512,1280]{1,0:T(8,128)(2,1)S(1)}, u32[]{:S(2)}, u32[]{:S(2)}) collective-permute-start(bf16[512,1280]{1,0:T(8,128)(2,1)S(1)} %convolution_convert_fusion.7), channel_id=1, source_target_pairs={{0,16},{8,24},{16,0},{24,8},{1,17},{9,25},{17,1},{25,9},{2,18},{10... | collective-permute-start | bytes 3932168 | tf_op jit(solution)/shard_map/ppermute | solution.py:35
  917.5 68.9 %collective-permute-start.51 = (bf16[512,1280]{1,0:T(8,128)(2,1)S(1)}, bf16[512,1280]{1,0:T(8,128)(2,1)S(1)}, u32[]{:S(2)}, u32[]{:S(2)}) collective-permute-start(bf16[512,1280]{1,0:T(8,128)(2,1)S(1)} %convolution_convert_fusion.8), channel_id=1, source_target_pairs={{0,8},{8,0},{16,24},{24,16},{1,9},{9,1},{17,25},{25,17},{2,10},{10... | collective-permute-start | bytes 3932168 | tf_op jit(solution)/shard_map/ppermute | solution.py:35
  920.2 40.9 %collective-permute-start.76 = (f32[2,2,160,160]{3,2,1,0:T(8,128)S(1)}, f32[2,2,160,160]{3,2,1,0:T(8,128)S(1)}, u32[]{:S(2)}, u32[]{:S(2)}) collective-permute-start(f32[2,2,160,160]{3,2,1,0:T(8,128)S(1)} %maximum_add_fusion.3), channel_id=1, source_target_pairs={{0,8},{8,0},{16,24},{24,16},{1,9},{9,1},{17,25},{25,17},{2,10},{10... | collective-permute-start | bytes 1228808 | tf_op jit(solution)/shard_map/ppermute | solution.py:35
  922.2 41.5 %collective-permute-start.58 = (bf16[640,256]{1,0:T(8,128)(2,1)S(1)}, bf16[640,256]{1,0:T(8,128)(2,1)S(1)}, u32[]{:S(2)}, u32[]{:S(2)}) collective-permute-start(bf16[640,256]{1,0:T(8,128)(2,1)S(1)} %get-tuple-element.160), channel_id=1, source_target_pairs={{0,16},{8,24},{16,0},{24,8},{1,17},{9,25},{17,1},{25,9},{2,18},{10... | collective-permute-start | bytes 983048 | tf_op jit(solution)/shard_map/ppermute | solution.py:35
  1008.4 39.5 %collective-permute-start.45 = (bf16[264,2048]{1,0:T(8,128)(2,1)S(1)}, bf16[264,2048]{1,0:T(8,128)(2,1)S(1)}, u32[]{:S(2)}, u32[]{:S(2)}) collective-permute-start(bf16[264,2048]{1,0:T(8,128)(2,1)S(1)} %dynamic-slice_convert_fusion), channel_id=1, source_target_pairs={{0,1},{1,0},{2,3},{3,2},{4,5},{5,4},{6,7},{7,6},{8,9},{9,8},{10,11... | collective-permute-start | bytes 3244040 | tf_op jit(solution)/shard_map/ppermute | solution.py:35
  (153 other events, 2985.0 us)
